TPU v7x, 32 devices: a whole 2x2x4 slice. The times are simulated.
32 devices in a mesh: px: 8 (over z, y), py: 4 (over x, core).
Axes of the slice: x: 2, y: 2, z: 4, core: 2. Of those that a mesh axis runs over, the one named last changes fastest.
Arguments:
- dofs: float32 [9, 20, 12288], P(None, None, ('px', 'py')), may hold values from -6 to 6
- star: float32 [3, 9, 9, 12288], P(None, None, None, ('px', 'py')), may hold values from -1.25 to 1.25
- flux_minus: float32 [4, 9, 9, 12288], P(None, None, None, ('px', 'py')), may hold values from -2 to 2
- flux_plus: float32 [4, 9, 9, 12288], P(None, None, None, ('px', 'py')), may hold values from -2 to 2
- stiffness: float32 [3, 20, 20], replicated, may hold values from -1.25 to 1.25
- project: float32 [4, 10, 20], replicated, may hold values from -1.25 to 1.25
- lift: float32 [4, 20, 10], replicated, may hold values from -1 to 1
- cluster: int32 [12288], P(('px', 'py')), may hold values from 0 to 1, as said below
- neighbour: int32 [4, 12288], P(None, ('px', 'py')), may hold values from 0 to 767
- neighbour_face: int32 [4, 12288], P(None, ('px', 'py')), may hold values from 0 to 3
- face_type: int32 [4, 12288], P(None, ('px', 'py')), may hold values from 0 to 2, as said below
- send_list: int32 [4, 3072], P(None, ('px', 'py')), may hold values from 0 to 383
Outputs:
- new_dofs: float32 [9, 20, 12288], P(None, None, ('px', 'py'))
Inputs may be any that keep to these rules, and one draw needn't show every extreme that they name: 0 is the fast cluster (two substeps of h), 1 the slow one (one step of 2 h); at most 192 of a partition's 384 elements are in cluster 0, and some partition has exactly 192. `neighbour`: below 384: a local element; from 384 on: a ghost in the order of the statement. Used only on faces of type 0. `face_type`: 0 an interior face, 1 a free surface, 2 an absorbing face. `send_list`: local element indices of the partition.
All inputs are finite; a program needn't handle non-finite values.
Results may differ from a plain program's by a relative error of at most 0.0003.
Values sent between devices are 32-bit elements; how exact they have to be, the bound alone decides.
No kernel may reach another device: no remote copies, remote signals or barrier semaphores. Data moves between devices by JAX's collectives and lax.ppermute only.
A program may use at most 64 MiB of HBM per device.

v0:
```python
import functools
import math

import jax
import jax.numpy as jnp
from jax import lax
from jax.experimental import pallas as pl
from jax.experimental.pallas import tpu as pltpu
from jax.sharding import PartitionSpec as P

f32, bf16 = jnp.float32, jnp.bfloat16
step_length = 0.5
LANES = 128
DIRS = 4


def weights_of(lower, upper):
    return [
        (upper ** (m + 1) - lower ** (m + 1)) / math.factorial(m + 1) for m in range(4)
    ]


def iota(shape, dim):
    return lax.broadcasted_iota(jnp.int32, shape, dim)


def split(x):
    high = x.astype(bf16)
    return high, (x - high.astype(f32)).astype(bf16)


def triple(x):
    high = x.astype(bf16).astype(f32)
    return jnp.concatenate([high, x - high, high], axis=0).astype(bf16)


def pad_rows(x, rows):
    return jnp.concatenate([x, x[2 * x.shape[0] - rows :]], axis=0)


def spread(matrix, rep, transposed):
    dims = (((0,) if transposed else (1,), (0,)), ((), ()))
    high, low = split(matrix)
    return [
        lax.dot_general(part, rep, dims, preferred_element_type=f32)
        for part in (high, low)
    ]


def block_weights(matrix, inner, copies, transposed):
    count = matrix.shape[0] if transposed else matrix.shape[1]
    width = 3 * copies * inner
    rep = (iota((count, width), 1) % inner == iota((count, width), 0)).astype(bf16)
    high, low = spread(matrix, rep, transposed)
    col = iota(high.shape, 1)
    both = jnp.where(col < 2 * copies * inner, high, low)
    owner = (col % (copies * inner)) // inner
    return [jnp.where(owner == q, both, 0.0) for q in range(copies)]


def series_weights(stiff_ref, rows, transposed):
    out = []
    for c in range(3):
        for block in block_weights(stiff_ref[c], rows, 3, transposed):
            out.append(pad_rows(block, rows))
    return jnp.concatenate(out, axis=0).astype(bf16)


def stacked(ref, first, count):
    return jnp.concatenate([ref[first + i] for i in range(count)], axis=0)


def star_mix(star_ref, t_ref, lane, quantities):
    rows = t_ref.shape[1]
    acc = [None] * quantities
    for c in range(3):
        for q in range(quantities):
            t = t_ref[c * quantities + q, :, lane]
            for p in range(quantities):
                term = jnp.broadcast_to(star_ref[p, q, c : c + 1, lane], (rows, LANES)) * t
                acc[p] = term if acc[p] is None else acc[p] + term
    return acc


def lane_tiles(n, body):
    def one(tile, carry):
        body(pl.ds(pl.multiple_of(tile * LANES, LANES), LANES))
        return carry

    lax.fori_loop(0, n // LANES, one, 0)


def stiff_products(w_ref, v_ref, t_ref, quantities):
    rows = v_ref.shape[1]
    for g in range(quantities // 3):
        x = triple(stacked(v_ref, 3 * g, 3))
        t = jnp.dot(w_ref[...], x, preferred_element_type=f32)
        for c in range(3):
            for i in range(3):
                start = (3 * c + i) * rows
                t_ref[c * quantities + 3 * g + i] = t[start : start + rows]


def series(w_ref, v_ref, t_ref, star_ref, sums):
    quantities = v_ref.shape[0]
    for ref, weights in sums:
        for q in range(quantities):
            ref[q] = weights[0] * v_ref[q]
    for m in range(1, 4):
        stiff_products(w_ref, v_ref, t_ref, quantities)

        def tile(lane, m=m):
            acc = star_mix(star_ref, t_ref, lane, quantities)
            for p in range(quantities):
                value = -acc[p]
                if m < 3:
                    v_ref[p, :, lane] = value
                for ref, weights in sums:
                    ref[p, :, lane] += weights[m] * value

        lane_tiles(v_ref.shape[2], tile)


def pack_sends(buffer_ref, lists_ref, out_ref, parity):
    quantities, rows, n = buffer_ref.shape
    high, low = split(stacked(buffer_ref, 0, quantities))
    both = jnp.concatenate([high, low], axis=0)
    count = lists_ref.shape[1]
    wanted = lists_ref[...]
    for e in range(DIRS):
        axis = e // 2
        even, odd = (1, 0) if e % 2 == 0 else (0, 1)
        row = jnp.where(
            parity[axis] == 0,
            wanted[2 * axis + even : 2 * axis + even + 1],
            wanted[2 * axis + odd : 2 * axis + odd + 1],
        )
        pick = (iota((n, count), 0) == row).astype(bf16)
        got = jnp.dot(both, pick, preferred_element_type=f32)
        total = got[: quantities * rows] + got[quantities * rows :]
        for q in range(quantities):
            out_ref[e, q] = total[q * rows : (q + 1) * rows]


def parities(axes):
    return [lax.rem(lax.axis_index(axis), 2) for axis in axes]


def predict_kernel(axes, dofs_ref, star_ref, stiff_ref, lists_ref, first_ref, late_ref, send_ref, w_ref, v_ref, t_ref):
    h = step_length
    rows = first_ref.shape[1]
    w_ref[...] = series_weights(stiff_ref, rows, False)
    for q in range(dofs_ref.shape[0]):
        v_ref[q] = pad_rows(dofs_ref[q], rows)
    sums = [(first_ref, weights_of(0.0, h)), (late_ref, weights_of(h, 2 * h))]
    series(w_ref, v_ref, t_ref, star_ref, sums)
    pack_sends(first_ref, lists_ref, send_ref, parities(axes))


def effective(type_ref, near_ref, face_ref):
    kind = type_ref[...]
    n = kind.shape[1]
    index = jnp.where(kind == 0, near_ref[...], jnp.where(kind == 1, iota(kind.shape, 1), -1))
    source = jnp.where(kind == 0, face_ref[...], jnp.where(kind == 1, iota(kind.shape, 0), 0))
    return index, source


def across_weights(project_ref):
    faces_basis, faces, count = project_ref.shape
    main = (count // 8) * 8
    rest = count - main
    width = faces * count
    col = iota((count, 3 * width), 1) % width
    basis = jnp.where(col < faces * main, col % main, main + (col - faces * main) % rest)
    rep = (basis == iota((count, 3 * width), 0)).astype(bf16)
    tall = faces_basis * faces
    grow = (iota((tall, faces_basis), 0) // faces == iota((tall, faces_basis), 1)).astype(bf16)
    col = iota((tall, 3 * width), 1)
    inner = col % width
    owner = jnp.where(inner < faces * main, inner // main, (inner - faces * main) // rest)
    mine = owner == iota((tall, 3 * width), 0) % faces
    out = []
    for g in range(faces):
        matrix = jnp.concatenate([project_ref[b, g : g + 1] for b in range(faces_basis)], axis=0)
        high, low = spread(matrix, rep, False)
        high = jnp.dot(grow, high.astype(bf16), preferred_element_type=f32)
        low = jnp.dot(grow, low.astype(bf16), preferred_element_type=f32)
        out.append(jnp.where(mine, jnp.where(col < 2 * width, high, low), 0.0))
    return jnp.concatenate(out, axis=0).astype(bf16)


def across_operand(picked, q, rows, height):
    parts = []
    for part in range(2):
        start = part * height + q * rows
        main = [ref[start : start + 16] for ref in picked]
        rest = [ref[start + 16 : start + 24] for ref in picked]
        lower = iota(rest[0].shape, 0) < 4
        parts.append(
            jnp.concatenate(
                main + [jnp.where(lower, rest[0], rest[1]), jnp.where(lower, rest[2], rest[3])], axis=0
            )
        )
    return jnp.concatenate([parts[0], parts[1], parts[0]], axis=0).astype(bf16)


def across_traces(w_ref, picked, source, quantities, rows, store):
    height = quantities * rows
    faces = len(picked)
    tall = w_ref.shape[0] // faces
    wide = jnp.concatenate([source] * (tall // faces), axis=0)
    tests = [wide == g for g in range(faces - 1)]
    for q in range(quantities):
        z = jnp.dot(
            w_ref[...], across_operand(picked, q, rows, height), preferred_element_type=f32
        )
        value = z[(faces - 1) * tall :]
        for g in reversed(range(faces - 1)):
            value = jnp.where(tests[g], z[g * tall : (g + 1) * tall], value)
        store(q, value)


def flux_mix(flux_ref, trace_ref, lane, start):
    quantities, tall = trace_ref.shape[0], trace_ref.shape[1]
    faces = flux_ref.shape[2]
    acc = list(start)
    for q in range(quantities):
        t = trace_ref[q, :, lane]
        for p in range(quantities):
            factor = flux_ref[p, q, :, lane]
            term = jnp.concatenate([factor] * (tall // faces), axis=0) * t
            acc[p] = term if acc[p] is None else acc[p] + term
    return acc


def own_kernel(own_ref, star_ref, minus_ref, stiff_ref, project_ref, near_ref, face_ref, type_ref,
               part_ref, g_ref, across_ref, w_ref, wa_ref, trace_ref, t_ref, picked_ref, pick_ref):
    quantities, rows, n = own_ref.shape
    faces_basis, faces, count = project_ref.shape
    tall = faces_basis * faces
    flat = jnp.concatenate([project_ref[b] for b in range(faces_basis)], axis=0)
    w_ref[: 9 * rows] = series_weights(stiff_ref, rows, True)
    w_ref[9 * rows :] = jnp.concatenate(block_weights(flat, rows, 3, False), axis=0).astype(bf16)
    wa_ref[...] = across_weights(project_ref)
    for g in range(quantities // 3):
        x = triple(stacked(own_ref, 3 * g, 3))
        t = jnp.dot(w_ref[...], x, preferred_element_type=f32)
        for c in range(3):
            for i in range(3):
                start = (3 * c + i) * rows
                t_ref[c * quantities + 3 * g + i] = t[start : start + rows]
        for i in range(3):
            start = 9 * rows + i * tall
            trace_ref[3 * g + i] = t[start : start + tall]

    index, source = effective(type_ref, near_ref, face_ref)
    high, low = split(stacked(own_ref, 0, quantities))
    both = jnp.concatenate([high, low], axis=0)
    for f in range(faces):
        pick_ref[...] = (iota((n, n), 0) == index[f : f + 1]).astype(bf16)
        picked_ref[f] = jnp.dot(both, pick_ref[...], preferred_element_type=f32)

    def keep(q, value):
        across_ref[q] = value

    across_traces(wa_ref, [picked_ref.at[f] for f in range(faces)], source, quantities, rows, keep)

    def tile(lane):
        acc = star_mix(star_ref, t_ref, lane, quantities)
        for p in range(quantities):
            part_ref[p, :, lane] = acc[p]
        acc = flux_mix(minus_ref, trace_ref, lane, [None] * quantities)
        for p in range(quantities):
            g_ref[p, :, lane] = acc[p]

    lane_tiles(n, tile)


def lift_weights(lift_ref, rows):
    faces_basis = lift_ref.shape[0]
    flat = jnp.concatenate([lift_ref[b] for b in range(faces_basis)], axis=0)
    blocks = block_weights(flat, flat.shape[0], 2, True)
    return jnp.concatenate([pad_rows(block, rows) for block in blocks], axis=0).astype(bf16)


def ghost_part(axes, got_refs, plus_ref, project_ref, lift_ref, near_ref, face_ref, type_ref,
               part_ref, g_ref, across_ref, wa_ref, wl_ref, picked_ref, pick_ref, trace_ref, flux_ref, emit):
    quantities, rows, n = part_ref.shape
    faces = project_ref.shape[1]
    count = got_refs[0].shape[2]
    wa_ref[...] = across_weights(project_ref)
    wl_ref[...] = lift_weights(lift_ref, rows)
    index, source = effective(type_ref, near_ref, face_ref)
    parity = parities(axes)
    ghost = index - n
    block = ghost // count
    axis_parity = jnp.where(block < 2, parity[0], parity[1])
    slot = (block // 2) * 2 + jnp.where(block % 2 == 1, axis_parity, 1 - axis_parity)
    column = jnp.where(ghost >= 0, slot * LANES + ghost % count, -1)
    operands = []
    for e in range(DIRS):
        high, low = split(stacked(got_refs[e], 0, quantities))
        both = jnp.concatenate([high, low], axis=0)
        empty = jnp.zeros((both.shape[0], LANES - count), bf16)
        operands.append(jnp.concatenate([both, empty], axis=1))
    operand = jnp.concatenate(operands, axis=1)
    for f in range(faces):
        pick_ref[...] = (iota((DIRS * LANES, n), 0) == column[f : f + 1]).astype(bf16)
        picked_ref[f] = jnp.dot(operand, pick_ref[...], preferred_element_type=f32)

    def keep(q, value):
        trace_ref[q] = across_ref[q] + value

    across_traces(wa_ref, [picked_ref.at[f] for f in range(faces)], source, quantities, rows, keep)

    def tile(lane):
        acc = flux_mix(plus_ref, trace_ref, lane, [g_ref[p, :, lane] for p in range(quantities)])
        for p in range(quantities):
            flux_ref[p, :, lane] = acc[p]

    lane_tiles(n, tile)
    for pair in range(0, quantities, 2):
        two = pair + 1 < quantities
        x = jnp.concatenate(
            [flux_ref[pair], flux_ref[pair + 1] if two else jnp.zeros(flux_ref.shape[1:], f32)], axis=0
        )
        lifted = jnp.dot(wl_ref[...], triple(x), preferred_element_type=f32)
        emit(pair, part_ref[pair] - lifted[:rows])
        if two:
            emit(pair + 1, part_ref[pair + 1] - lifted[rows:])


def middle_kernel(axes, got0, got1, got2, got3, plus_ref, project_ref, lift_ref, near_ref, face_ref, type_ref,
                  part_ref, g_ref, across_ref, dofs_ref, star_ref, stiff_ref, cluster_ref, late_ref, lists_ref,
                  midway_ref, second_ref, send_ref,
                  wa_ref, wl_ref, picked_ref, pick_ref, trace_ref, flux_ref, w_ref, v_ref, t_ref):
    rows = part_ref.shape[1]
    quantities = part_ref.shape[0]

    def emit(q, change):
        value = pad_rows(dofs_ref[q], rows) + change
        midway_ref[q] = value
        v_ref[q] = value

    ghost_part(axes, [got0, got1, got2, got3], plus_ref, project_ref, lift_ref, near_ref, face_ref, type_ref,
               part_ref, g_ref, across_ref, wa_ref, wl_ref, picked_ref, pick_ref, trace_ref, flux_ref, emit)
    w_ref[...] = series_weights(stiff_ref, rows, False)
    series(w_ref, v_ref, t_ref, star_ref, [(second_ref, weights_of(0.0, step_length))])
    fast = cluster_ref[...] == 0
    for q in range(quantities):
        second_ref[q] = jnp.where(fast, second_ref[q], late_ref[q])
    pack_sends(second_ref, lists_ref, send_ref, parities(axes))


def finish_kernel(axes, got0, got1, got2, got3, plus_ref, project_ref, lift_ref, near_ref, face_ref, type_ref,
                  part_ref, g_ref, across_ref, midway_ref, out_ref,
                  wa_ref, wl_ref, picked_ref, pick_ref, trace_ref, flux_ref):
    count = out_ref.shape[1]

    def emit(q, change):
        out_ref[q] = (midway_ref[q] + change)[:count]

    ghost_part(axes, [got0, got1, got2, got3], plus_ref, project_ref, lift_ref, near_ref, face_ref, type_ref,
               part_ref, g_ref, across_ref, wa_ref, wl_ref, picked_ref, pick_ref, trace_ref, flux_ref, emit)


def call(kernel, name, args, outs, scratch, flops):
    spec = pl.BlockSpec(memory_space=pltpu.VMEM)
    size = sum(4 * math.prod(a.shape) for a in list(args) + list(outs))
    return pl.pallas_call(
        kernel,
        out_shape=[jax.ShapeDtypeStruct(s.shape, s.dtype) for s in outs],
        in_specs=[spec] * len(args),
        out_specs=[spec] * len(outs),
        scratch_shapes=scratch,
        cost_estimate=pl.CostEstimate(flops=flops, bytes_accessed=size, transcendentals=0),
        name=name,
    )(*args)


def exchange(block, axis, offset):
    count = lax.axis_size(axis)
    route = []
    for i in range(offset, count - 1, 2):
        route += [(i, i + 1), (i + 1, i)]
    return lax.ppermute(block, axis, route)


def swap(sends):
    return [
        exchange(sends[0], "px", 0),
        exchange(sends[1], "px", 1),
        exchange(sends[2], "py", 0),
        exchange(sends[3], "py", 1),
    ]


def per_device(dofs, star, flux_minus, flux_plus, stiffness, project, lift, cluster, neighbour, neighbour_face,
               face_type, send_list):
    axes = ("px", "py")
    quantities, count, n = dofs.shape
    faces, faces_basis = project.shape[:2]
    rows = 8 * pl.cdiv(count, 8)
    tall = faces * faces_basis
    width = send_list.shape[1]
    star = jnp.transpose(star, (1, 2, 0, 3))
    minus = jnp.transpose(flux_minus, (1, 2, 0, 3))
    plus = jnp.transpose(flux_plus, (1, 2, 0, 3))
    project = jnp.transpose(project, (1, 0, 2))
    lift = jnp.transpose(lift, (2, 0, 1))
    cluster = cluster.reshape(1, n)

    field = jax.ShapeDtypeStruct((quantities, rows, n), f32)
    traces = jax.ShapeDtypeStruct((quantities, tall, n), f32)
    sends = jax.ShapeDtypeStruct((DIRS, quantities, rows, width), f32)
    series_w = pltpu.VMEM((9 * rows, 9 * rows), bf16)
    v_field = pltpu.VMEM((quantities, rows, n), f32)
    t_field = pltpu.VMEM((3 * quantities, rows, n), f32)
    t_trace = pltpu.VMEM((quantities, tall, n), f32)
    across_w = pltpu.VMEM((faces * tall, 3 * faces * count), bf16)
    lift_w = pltpu.VMEM((2 * rows, 6 * tall), bf16)
    picked = pltpu.VMEM((faces, 2 * quantities * rows, n), f32)

    first, late, out = call(
        functools.partial(predict_kernel, axes), "predict", (dofs, star, stiffness, send_list),
        (field, field, sends), [series_w, v_field, t_field], 10_000_000)

    def own(buffer, name):
        return call(
            own_kernel, name, (buffer, star, minus, stiffness, project, neighbour, neighbour_face, face_type),
            (field, traces, traces),
            [pltpu.VMEM((9 * rows + 3 * tall, 9 * rows), bf16), across_w, t_trace, t_field, picked,
             pltpu.VMEM((n, n), bf16)], 10_000_000)

    ghost_scratch = [across_w, lift_w, picked, pltpu.VMEM((DIRS * LANES, n), bf16), t_trace, t_trace]
    got = swap([out[e] for e in range(DIRS)])
    part, g, across = own(first, "own_first")
    midway, second, out = call(
        functools.partial(middle_kernel, axes), "middle",
        (*got, plus, project, lift, neighbour, neighbour_face, face_type, part, g, across, dofs, star, stiffness,
         cluster, late, send_list),
        (field, field, sends), ghost_scratch + [series_w, v_field, t_field], 10_000_000)
    got = swap([out[e] for e in range(DIRS)])
    part, g, across = own(second, "own_second")
    (result,) = call(
        functools.partial(finish_kernel, axes), "finish",
        (*got, plus, project, lift, neighbour, neighbour_face, face_type, part, g, across, midway),
        (jax.ShapeDtypeStruct((quantities, count, n), f32),), ghost_scratch, 10_000_000)
    return result


def solution(mesh):
    both = ("px", "py")
    in_specs = (
        P(None, None, both),
        P(None, None, None, both),
        P(None, None, None, both),
        P(None, None, None, both),
        P(),
        P(),
        P(),
        P(both),
        P(None, both),
        P(None, both),
        P(None, both),
        P(None, both),
    )
    return jax.shard_map(
        per_device, mesh=mesh, in_specs=in_specs, out_specs=P(None, None, both), check_vma=False
    )
```

profile of v0, /device:TPU:0, one launch (start us, length us, event | category | flops | bytes accessed | tf_op | source)
XLA Modules:
  0.0 55.7 jit_solution(42088547095426901)
XLA Ops:
  0.0 6.1 %predict.1 = (f32[9,24,384]{2,1,0:T(8,128)}, f32[9,24,384]{2,1,0:T(8,128)}, f32[4,9,24,96]{3,2,1,0:T(8,128)}) custom-call(f32[9,20,384]{2,1,0:T(8,128)} %dofs_ref.3, f32[9,9,3,384]{3,2,1,0:T(4,128)} %bitcast.21, f32[3,20,20]{2,1,0:T(8,128)} %stiff_ref.7, s32[4,96]{1,0:T(4,128)} %lists_ref.3), custom_call_target="tpu_custom_call" | custom-call | flops 10000000 | bytes 1651392 | tf_op jit(solution)/shard_map/predict/pallas_call | solution.py:370
  6.1 1.1 %slice_bitcast_fusion.4 = (f32[9,24,96]{2,1,0:T(8,128)S(1)}, f32[9,24,96]{2,1,0:T(8,128)S(1)}, f32[9,24,96]{2,1,0:T(8,128)S(1)}, f32[9,24,96]{2,1,0:T(8,128)S(1)}) fusion(f32[4,9,24,96]{3,2,1,0:T(8,128)} %get-tuple-element.17), kind=kLoop, calls=%fused_computation.4 | loop fusion | bytes 663552 | tf_op jit(solution)/shard_map/squeeze | solution.py:436
  7.2 0.7 %collective-permute-start.3 = (f32[9,24,96]{2,1,0:T(8,128)S(1)}, f32[9,24,96]{2,1,0:T(8,128)S(1)}, u32[]{:S(2)}, u32[]{:S(2)}) collective-permute-start(f32[9,24,96]{2,1,0:T(8,128)S(1)} %get-tuple-element.33), channel_id=1, source_target_pairs={{1,2},{2,1},{5,6},{6,5},{9,10},{10,9},{13,14},{14,13},{17,18},{18,... | collective-permute-start | bytes 248840 | tf_op jit(solution)/shard_map/ppermute | solution.py:386
  7.8 0.0 copy-start.8
  7.8 4.4 %collective-permute-start.2 = (f32[9,24,96]{2,1,0:T(8,128)S(1)}, f32[9,24,96]{2,1,0:T(8,128)S(1)}, u32[]{:S(2)}, u32[]{:S(2)}) collective-permute-start(f32[9,24,96]{2,1,0:T(8,128)S(1)} %get-tuple-element.34), channel_id=1, source_target_pairs={{0,1},{1,0},{2,3},{3,2},{4,5},{5,4},{6,7},{7,6},{8,9},{9,8},{10,11... | collective-permute-start | bytes 248840 | tf_op jit(solution)/shard_map/ppermute | solution.py:386
  12.2 0.7 %collective-permute-start.1 = (f32[9,24,96]{2,1,0:T(8,128)S(1)}, f32[9,24,96]{2,1,0:T(8,128)S(1)}, u32[]{:S(2)}, u32[]{:S(2)}) collective-permute-start(f32[9,24,96]{2,1,0:T(8,128)S(1)} %get-tuple-element.35), channel_id=1, source_target_pairs={{4,8},{8,4},{12,16},{16,12},{20,24},{24,20},{5,9},{9,5},{13,17},{1... | collective-permute-start | bytes 248840 | tf_op jit(solution)/shard_map/ppermute | solution.py:386
  12.9 4.3 %collective-permute-start = (f32[9,24,96]{2,1,0:T(8,128)S(1)}, f32[9,24,96]{2,1,0:T(8,128)S(1)}, u32[]{:S(2)}, u32[]{:S(2)}) collective-permute-start(f32[9,24,96]{2,1,0:T(8,128)S(1)} %get-tuple-element.36), channel_id=1, source_target_pairs={{0,4},{4,0},{8,12},{12,8},{16,20},{20,16},{24,28},{28,24},{1,5},{5... | collective-permute-start | bytes 248840 | tf_op jit(solution)/shard_map/ppermute | solution.py:386
  17.2 0.6 %reshape.3.cluster_ref = s32[1,384]{1,0:T(1,128)} reshape(s32[384]{0:T(512)S(1)} %copy-done.8) | data formatting | bytes 3072 | tf_op jit(solution)/shard_map/reshape | solution.py:411
  17.8 6.2 %own_first.1 = (f32[9,24,384]{2,1,0:T(8,128)}, f32[9,40,384]{2,1,0:T(8,128)}, f32[9,40,384]{2,1,0:T(8,128)}) custom-call(f32[9,24,384]{2,1,0:T(8,128)} %get-tuple-element.18.own_ref, f32[9,9,3,384]{3,2,1,0:T(4,128)} %bitcast.22, f32[9,9,4,384]{3,2,1,0:T(4,128)} %bitcast.27, f32[3,20,20]{2,1,0:T(8,128)} %stiff_ref.7, f32[10,4,20]{2,1,0:T(4,128)} %bitcast.29, ...), custom_call_target="tpu_custom_call" | custom-call | flops 10000000 | bytes 2666816 | tf_op jit(solution)/shard_map/own_first/pallas_call | solution.py:370
  24.0 0.0 collective-permute-done.3.got3
  24.0 0.0 collective-permute-done.2.got2
  24.0 0.0 collective-permute-done.1.got1
  24.1 0.0 collective-permute-done.got0
  24.1 0.6 %copy-done = f32[9,24,96]{2,1,0:T(8,128)} copy-done((f32[9,24,96]{2,1,0:T(8,128)}, f32[9,24,96]{2,1,0:T(8,128)S(1)}, u32[]{:S(2)}) %copy-start) | copy-done | bytes 82968
  24.7 0.0 copy-done.1
  24.7 0.1 copy-done.3
  24.8 0.0 copy-done.5
  24.8 10.1 %middle.1 = (f32[9,24,384]{2,1,0:T(8,128)}, f32[9,24,384]{2,1,0:T(8,128)}, f32[4,9,24,96]{3,2,1,0:T(8,128)}) custom-call(f32[9,24,96]{2,1,0:T(8,128)} %copy-done.5, f32[9,24,96]{2,1,0:T(8,128)} %copy-done.3, f32[9,24,96]{2,1,0:T(8,128)} %copy-done.1, f32[9,24,96]{2,1,0:T(8,128)} %copy-done, f32[9,9,4,384]{3,2,1,0:T(4,128)} %bitcast.25, ...), custom_call_target="tpu_custom_call" | custom-call | flops 10000000 | bytes 4276672 | tf_op jit(solution)/shard_map/middle/pallas_call | solution.py:370
  34.9 1.1 %slice_bitcast_fusion = (f32[9,24,96]{2,1,0:T(8,128)S(1)}, f32[9,24,96]{2,1,0:T(8,128)S(1)}, f32[9,24,96]{2,1,0:T(8,128)S(1)}, f32[9,24,96]{2,1,0:T(8,128)S(1)}) fusion(f32[4,9,24,96]{3,2,1,0:T(8,128)} %get-tuple-element.23), kind=kLoop, calls=%fused_computation | loop fusion | bytes 663552 | tf_op jit(solution)/shard_map/squeeze | solution.py:443
  36.0 0.7 %collective-permute-start.7 = (f32[9,24,96]{2,1,0:T(8,128)S(1)}, f32[9,24,96]{2,1,0:T(8,128)S(1)}, u32[]{:S(2)}, u32[]{:S(2)}) collective-permute-start(f32[9,24,96]{2,1,0:T(8,128)S(1)} %get-tuple-element.29), channel_id=1, source_target_pairs={{1,2},{2,1},{5,6},{6,5},{9,10},{10,9},{13,14},{14,13},{17,18},{18,... | collective-permute-start | bytes 248840 | tf_op jit(solution)/shard_map/ppermute | solution.py:386
  36.6 1.3 %collective-permute-start.6 = (f32[9,24,96]{2,1,0:T(8,128)S(1)}, f32[9,24,96]{2,1,0:T(8,128)S(1)}, u32[]{:S(2)}, u32[]{:S(2)}) collective-permute-start(f32[9,24,96]{2,1,0:T(8,128)S(1)} %get-tuple-element.30), channel_id=1, source_target_pairs={{0,1},{1,0},{2,3},{3,2},{4,5},{5,4},{6,7},{7,6},{8,9},{9,8},{10,11... | collective-permute-start | bytes 248840 | tf_op jit(solution)/shard_map/ppermute | solution.py:386
  38.0 0.8 %collective-permute-start.5 = (f32[9,24,96]{2,1,0:T(8,128)S(1)}, f32[9,24,96]{2,1,0:T(8,128)S(1)}, u32[]{:S(2)}, u32[]{:S(2)}) collective-permute-start(f32[9,24,96]{2,1,0:T(8,128)S(1)} %get-tuple-element.31), channel_id=1, source_target_pairs={{4,8},{8,4},{12,16},{16,12},{20,24},{24,20},{5,9},{9,5},{13,17},{1... | collective-permute-start | bytes 248840 | tf_op jit(solution)/shard_map/ppermute | solution.py:386
  38.8 4.4 %collective-permute-start.4 = (f32[9,24,96]{2,1,0:T(8,128)S(1)}, f32[9,24,96]{2,1,0:T(8,128)S(1)}, u32[]{:S(2)}, u32[]{:S(2)}) collective-permute-start(f32[9,24,96]{2,1,0:T(8,128)S(1)} %get-tuple-element.32), channel_id=1, source_target_pairs={{0,4},{4,0},{8,12},{12,8},{16,20},{20,16},{24,28},{28,24},{1,5},{5... | collective-permute-start | bytes 248840 | tf_op jit(solution)/shard_map/ppermute | solution.py:386
  43.2 6.2 %own_second.1 = (f32[9,24,384]{2,1,0:T(8,128)}, f32[9,40,384]{2,1,0:T(8,128)}, f32[9,40,384]{2,1,0:T(8,128)}) custom-call(f32[9,24,384]{2,1,0:T(8,128)} %get-tuple-element.24.own_ref, f32[9,9,3,384]{3,2,1,0:T(4,128)} %bitcast.24, f32[9,9,4,384]{3,2,1,0:T(4,128)} %bitcast.28, f32[3,20,20]{2,1,0:T(8,128)} %stiff_ref.7, f32[10,4,20]{2,1,0:T(4,128)} %bitcast.31, ...), custom_call_target="tpu_custom_call" | custom-call | flops 10000000 | bytes 2666816 | tf_op jit(solution)/shard_map/own_second/pallas_call | solution.py:370
  49.4 0.0 collective-permute-done.7.got3
  49.4 0.0 collective-permute-done.6.got2
  49.4 0.0 collective-permute-done.4.got0
  49.4 0.6 %copy-done.2 = f32[9,24,96]{2,1,0:T(8,128)} copy-done((f32[9,24,96]{2,1,0:T(8,128)}, f32[9,24,96]{2,1,0:T(8,128)S(1)}, u32[]{:S(2)}) %copy-start.2) | copy-done | bytes 82968
  50.0 0.1 copy-done.4
  50.1 0.0 copy-done.6
  50.1 0.1 copy-done.7
  50.2 5.5 %finish.1 = f32[9,20,384]{2,1,0:T(8,128)} custom-call(f32[9,24,96]{2,1,0:T(8,128)} %copy-done.7, f32[9,24,96]{2,1,0:T(8,128)} %copy-done.6, f32[9,24,96]{2,1,0:T(8,128)} %copy-done.4, f32[9,24,96]{2,1,0:T(8,128)} %copy-done.2, f32[9,9,4,384]{3,2,1,0:T(4,128)} %bitcast.26, f32[10,4,20]{2,1,0:T(4,128)} %bitcast.32, f32[10,4,20]{2,1,0:T(4,128)} %bitcast.34, ...), custom_call_target="tpu_custom_call" | custom-call | flops 10000000 | bytes 2900224 | tf_op jit(solution)/shard_map/finish/pallas_call | solution.py:370
  (10 shorter events, 0.0 us)
Async XLA Ops:
  7.2 16.9 %collective-permute-start.3 = (f32[9,24,96]{2,1,0:T(8,128)S(1)}, f32[9,24,96]{2,1,0:T(8,128)S(1)}, u32[]{:S(2)}, u32[]{:S(2)}) collective-permute-start(f32[9,24,96]{2,1,0:T(8,128)S(1)} %get-tuple-element.33), channel_id=1, source_target_pairs={{1,2},{2,1},{5,6},{6,5},{9,10},{10,9},{13,14},{14,13},{17,18},{18,... | collective-permute-start | bytes 248840 | tf_op jit(solution)/shard_map/ppermute | solution.py:386
  7.8 9.4 %copy-start.8 = (s32[384]{0:T(512)S(1)}, s32[384]{0:T(512)}, u32[]{:S(2)}) copy-start(s32[384]{0:T(512)} %param.19) | copy-start | bytes 4612
  7.8 16.2 %collective-permute-start.2 = (f32[9,24,96]{2,1,0:T(8,128)S(1)}, f32[9,24,96]{2,1,0:T(8,128)S(1)}, u32[]{:S(2)}, u32[]{:S(2)}) collective-permute-start(f32[9,24,96]{2,1,0:T(8,128)S(1)} %get-tuple-element.34), channel_id=1, source_target_pairs={{0,1},{1,0},{2,3},{3,2},{4,5},{5,4},{6,7},{7,6},{8,9},{9,8},{10,11... | collective-permute-start | bytes 248840 | tf_op jit(solution)/shard_map/ppermute | solution.py:386
  12.2 11.8 %collective-permute-start.1 = (f32[9,24,96]{2,1,0:T(8,128)S(1)}, f32[9,24,96]{2,1,0:T(8,128)S(1)}, u32[]{:S(2)}, u32[]{:S(2)}) collective-permute-start(f32[9,24,96]{2,1,0:T(8,128)S(1)} %get-tuple-element.35), channel_id=1, source_target_pairs={{4,8},{8,4},{12,16},{16,12},{20,24},{24,20},{5,9},{9,5},{13,17},{1... | collective-permute-start | bytes 248840 | tf_op jit(solution)/shard_map/ppermute | solution.py:386
  12.9 11.2 %collective-permute-start = (f32[9,24,96]{2,1,0:T(8,128)S(1)}, f32[9,24,96]{2,1,0:T(8,128)S(1)}, u32[]{:S(2)}, u32[]{:S(2)}) collective-permute-start(f32[9,24,96]{2,1,0:T(8,128)S(1)} %get-tuple-element.36), channel_id=1, source_target_pairs={{0,4},{4,0},{8,12},{12,8},{16,20},{20,16},{24,28},{28,24},{1,5},{5... | collective-permute-start | bytes 248840 | tf_op jit(solution)/shard_map/ppermute | solution.py:386
  24.0 0.6 %copy-start = (f32[9,24,96]{2,1,0:T(8,128)}, f32[9,24,96]{2,1,0:T(8,128)S(1)}, u32[]{:S(2)}) copy-start(f32[9,24,96]{2,1,0:T(8,128)S(1)} %collective-permute-done.3.got3) | copy-start | bytes 248836
  24.0 0.7 %copy-start.1 = (f32[9,24,96]{2,1,0:T(8,128)}, f32[9,24,96]{2,1,0:T(8,128)S(1)}, u32[]{:S(2)}) copy-start(f32[9,24,96]{2,1,0:T(8,128)S(1)} %collective-permute-done.2.got2) | copy-start | bytes 248836
  24.1 0.7 %copy-start.3 = (f32[9,24,96]{2,1,0:T(8,128)}, f32[9,24,96]{2,1,0:T(8,128)S(1)}, u32[]{:S(2)}) copy-start(f32[9,24,96]{2,1,0:T(8,128)S(1)} %collective-permute-done.1.got1) | copy-start | bytes 248836
  24.1 0.7 %copy-start.5 = (f32[9,24,96]{2,1,0:T(8,128)}, f32[9,24,96]{2,1,0:T(8,128)S(1)}, u32[]{:S(2)}) copy-start(f32[9,24,96]{2,1,0:T(8,128)S(1)} %collective-permute-done.got0) | copy-start | bytes 248836
  36.0 13.4 %collective-permute-start.7 = (f32[9,24,96]{2,1,0:T(8,128)S(1)}, f32[9,24,96]{2,1,0:T(8,128)S(1)}, u32[]{:S(2)}, u32[]{:S(2)}) collective-permute-start(f32[9,24,96]{2,1,0:T(8,128)S(1)} %get-tuple-element.29), channel_id=1, source_target_pairs={{1,2},{2,1},{5,6},{6,5},{9,10},{10,9},{13,14},{14,13},{17,18},{18,... | collective-permute-start | bytes 248840 | tf_op jit(solution)/shard_map/ppermute | solution.py:386
  36.6 12.7 %collective-permute-start.6 = (f32[9,24,96]{2,1,0:T(8,128)S(1)}, f32[9,24,96]{2,1,0:T(8,128)S(1)}, u32[]{:S(2)}, u32[]{:S(2)}) collective-permute-start(f32[9,24,96]{2,1,0:T(8,128)S(1)} %get-tuple-element.30), channel_id=1, source_target_pairs={{0,1},{1,0},{2,3},{3,2},{4,5},{5,4},{6,7},{7,6},{8,9},{9,8},{10,11... | collective-permute-start | bytes 248840 | tf_op jit(solution)/shard_map/ppermute | solution.py:386
  38.0 11.4 %collective-permute-start.5 = (f32[9,24,96]{2,1,0:T(8,128)S(1)}, f32[9,24,96]{2,1,0:T(8,128)S(1)}, u32[]{:S(2)}, u32[]{:S(2)}) collective-permute-start(f32[9,24,96]{2,1,0:T(8,128)S(1)} %get-tuple-element.31), channel_id=1, source_target_pairs={{4,8},{8,4},{12,16},{16,12},{20,24},{24,20},{5,9},{9,5},{13,17},{1... | collective-permute-start | bytes 248840 | tf_op jit(solution)/shard_map/ppermute | solution.py:386
  38.8 10.6 %collective-permute-start.4 = (f32[9,24,96]{2,1,0:T(8,128)S(1)}, f32[9,24,96]{2,1,0:T(8,128)S(1)}, u32[]{:S(2)}, u32[]{:S(2)}) collective-permute-start(f32[9,24,96]{2,1,0:T(8,128)S(1)} %get-tuple-element.32), channel_id=1, source_target_pairs={{0,4},{4,0},{8,12},{12,8},{16,20},{20,16},{24,28},{28,24},{1,5},{5... | collective-permute-start | bytes 248840 | tf_op jit(solution)/shard_map/ppermute | solution.py:386
  49.4 0.6 %copy-start.2 = (f32[9,24,96]{2,1,0:T(8,128)}, f32[9,24,96]{2,1,0:T(8,128)S(1)}, u32[]{:S(2)}) copy-start(f32[9,24,96]{2,1,0:T(8,128)S(1)} %collective-permute-done.7.got3) | copy-start | bytes 248836
  49.4 0.7 %copy-start.4 = (f32[9,24,96]{2,1,0:T(8,128)}, f32[9,24,96]{2,1,0:T(8,128)S(1)}, u32[]{:S(2)}) copy-start(f32[9,24,96]{2,1,0:T(8,128)S(1)} %collective-permute-done.6.got2) | copy-start | bytes 248836
  49.4 0.7 %copy-start.6 = (f32[9,24,96]{2,1,0:T(8,128)}, f32[9,24,96]{2,1,0:T(8,128)S(1)}, u32[]{:S(2)}) copy-start(f32[9,24,96]{2,1,0:T(8,128)S(1)} %collective-permute-done.5.got1) | copy-start | bytes 248836
  49.4 0.7 %copy-start.7 = (f32[9,24,96]{2,1,0:T(8,128)}, f32[9,24,96]{2,1,0:T(8,128)S(1)}, u32[]{:S(2)}) copy-start(f32[9,24,96]{2,1,0:T(8,128)S(1)} %collective-permute-done.4.got0) | copy-start | bytes 248836
where the time goes:
time: 56 us; the launch traced here: 55.7 us
  Pallas kernels  34 us (61%)
  starting transfers between devices  17.3 us (31%)
  local copies, waits for them, and re-layouts  4.22 us (8%)
    pallas_call x5, Pallas kernels, call(): pl.pallas_call(kernel, out_shape=[jax.ShapeDtypeStruct(s.shape, s.dtype)...  34 us
    ppermute x8, starting transfers between devices, exchange(): return lax.ppermute(block, axis, route)  17.3 us
    squeeze x2, local copies, waits for them, and re-layouts, per_device(): got = swap([out[e] for e in range(DIRS)])  2.17 us
    unnamed x18, local copies, waits for them, and re-layouts  1.46 us
  transfers between devices with their start and end apart: 8, of which 0 were waited for; matrix products, arithmetic and copies ran while one was open for 1% of the time, Pallas kernels for 22%

commit v1 on v0

--- a/solution.py
+++ b/solution.py
@@ -90,26 +90,28 @@
     lax.fori_loop(0, n // LANES, one, 0)
 
 
-def stiff_products(w_ref, v_ref, t_ref, quantities):
-    rows = v_ref.shape[1]
+def stiff_products(w_ref, v_ref, t_ref, lane):
+    quantities, rows = v_ref.shape[:2]
     for g in range(quantities // 3):
-        x = triple(stacked(v_ref, 3 * g, 3))
-        t = jnp.dot(w_ref[...], x, preferred_element_type=f32)
+        x = jnp.concatenate([v_ref[3 * g + i, :, lane] for i in range(3)], axis=0)
+        t = jnp.dot(w_ref[...], triple(x), preferred_element_type=f32)
         for c in range(3):
             for i in range(3):
                 start = (3 * c + i) * rows
-                t_ref[c * quantities + 3 * g + i] = t[start : start + rows]
+                t_ref[c * quantities + 3 * g + i, :, lane] = t[start : start + rows]
 
 
 def series(w_ref, v_ref, t_ref, star_ref, sums):
-    quantities = v_ref.shape[0]
+    quantities, _, n = v_ref.shape
+    tiles = n // LANES
     for ref, weights in sums:
         for q in range(quantities):
             ref[q] = weights[0] * v_ref[q]
+    stiff_products(w_ref, v_ref, t_ref, pl.ds(0, n))
     for m in range(1, 4):
-        stiff_products(w_ref, v_ref, t_ref, quantities)
-
-        def tile(lane, m=m):
+
+        def tile(index, carry, m=m):
+            lane = pl.ds(pl.multiple_of(index * LANES, LANES), LANES)
             acc = star_mix(star_ref, t_ref, lane, quantities)
             for p in range(quantities):
                 value = -acc[p]
@@ -117,11 +119,14 @@
                     v_ref[p, :, lane] = value
                 for ref, weights in sums:
                     ref[p, :, lane] += weights[m] * value
-
-        lane_tiles(v_ref.shape[2], tile)
-
-
-def pack_sends(buffer_ref, lists_ref, out_ref, parity):
+            return carry
+
+        lax.fori_loop(0, tiles, tile, 0)
+        if m < 3:
+            stiff_products(w_ref, v_ref, t_ref, pl.ds(0, n))
+
+
+def pack_sends(buffer_ref, lists_ref, out_refs, parity):
     quantities, rows, n = buffer_ref.shape
     high, low = split(stacked(buffer_ref, 0, quantities))
     both = jnp.concatenate([high, low], axis=0)
@@ -139,22 +144,30 @@
         got = jnp.dot(both, pick, preferred_element_type=f32)
         total = got[: quantities * rows] + got[quantities * rows :]
         for q in range(quantities):
-            out_ref[e, q] = total[q * rows : (q + 1) * rows]
+            out_refs[e][q] = total[q * rows : (q + 1) * rows]
 
 
 def parities(axes):
     return [lax.rem(lax.axis_index(axis), 2) for axis in axes]
 
 
-def predict_kernel(axes, dofs_ref, star_ref, stiff_ref, lists_ref, first_ref, late_ref, send_ref, w_ref, v_ref, t_ref):
+def predict_kernel(axes, dofs_in, star_in, stiff_in, lists_in, first_ref, late_ref, s0, s1, s2, s3,
+                   w_ref, v_ref, t_ref, stiff_ref, dofs_ref, star_ref, lists_ref, sems):
     h = step_length
     rows = first_ref.shape[1]
+    pairs = [(stiff_in, stiff_ref), (dofs_in, dofs_ref), (star_in, star_ref), (lists_in, lists_ref)]
+    copies = [pltpu.make_async_copy(src, dst, sems.at[i]) for i, (src, dst) in enumerate(pairs)]
+    for copy in copies:
+        copy.start()
+    copies[0].wait()
     w_ref[...] = series_weights(stiff_ref, rows, False)
+    for copy in copies[1:]:
+        copy.wait()
     for q in range(dofs_ref.shape[0]):
         v_ref[q] = pad_rows(dofs_ref[q], rows)
     sums = [(first_ref, weights_of(0.0, h)), (late_ref, weights_of(h, 2 * h))]
     series(w_ref, v_ref, t_ref, star_ref, sums)
-    pack_sends(first_ref, lists_ref, send_ref, parities(axes))
+    pack_sends(first_ref, lists_ref, [s0, s1, s2, s3], parities(axes))
 
 
 def effective(type_ref, near_ref, face_ref):
@@ -233,8 +246,10 @@
     return acc
 
 
-def own_kernel(own_ref, star_ref, minus_ref, stiff_ref, project_ref, near_ref, face_ref, type_ref,
-               part_ref, g_ref, across_ref, w_ref, wa_ref, trace_ref, t_ref, picked_ref, pick_ref):
+def own_kernel(own_ref, star_ref, minus_in, stiff_ref, project_ref, near_ref, face_ref, type_ref,
+               part_ref, g_ref, across_ref, w_ref, wa_ref, trace_ref, t_ref, picked_ref, pick_ref, minus_ref, sem):
+    minus_copy = pltpu.make_async_copy(minus_in, minus_ref, sem)
+    minus_copy.start()
     quantities, rows, n = own_ref.shape
     faces_basis, faces, count = project_ref.shape
     tall = faces_basis * faces
@@ -264,6 +279,8 @@
         across_ref[q] = value
 
     across_traces(wa_ref, [picked_ref.at[f] for f in range(faces)], source, quantities, rows, keep)
+
+    minus_copy.wait()
 
     def tile(lane):
         acc = star_mix(star_ref, t_ref, lane, quantities)
@@ -331,9 +348,11 @@
 
 
 def middle_kernel(axes, got0, got1, got2, got3, plus_ref, project_ref, lift_ref, near_ref, face_ref, type_ref,
-                  part_ref, g_ref, across_ref, dofs_ref, star_ref, stiff_ref, cluster_ref, late_ref, lists_ref,
-                  midway_ref, second_ref, send_ref,
-                  wa_ref, wl_ref, picked_ref, pick_ref, trace_ref, flux_ref, w_ref, v_ref, t_ref):
+                  part_ref, g_ref, across_ref, dofs_ref, star_ref, stiff_ref, cluster_in, late_ref, lists_ref,
+                  midway_ref, second_ref, s0, s1, s2, s3,
+                  wa_ref, wl_ref, picked_ref, pick_ref, trace_ref, flux_ref, w_ref, v_ref, t_ref, cluster_ref, sem):
+    cluster_copy = pltpu.make_async_copy(cluster_in, cluster_ref, sem)
+    cluster_copy.start()
     rows = part_ref.shape[1]
     quantities = part_ref.shape[0]
 
@@ -346,10 +365,11 @@
                part_ref, g_ref, across_ref, wa_ref, wl_ref, picked_ref, pick_ref, trace_ref, flux_ref, emit)
     w_ref[...] = series_weights(stiff_ref, rows, False)
     series(w_ref, v_ref, t_ref, star_ref, [(second_ref, weights_of(0.0, step_length))])
-    fast = cluster_ref[...] == 0
+    cluster_copy.wait()
+    fast = cluster_ref[...][None, :] == 0
     for q in range(quantities):
         second_ref[q] = jnp.where(fast, second_ref[q], late_ref[q])
-    pack_sends(second_ref, lists_ref, send_ref, parities(axes))
+    pack_sends(second_ref, lists_ref, [s0, s1, s2, s3], parities(axes))
 
 
 def finish_kernel(axes, got0, got1, got2, got3, plus_ref, project_ref, lift_ref, near_ref, face_ref, type_ref,
@@ -364,18 +384,20 @@
                part_ref, g_ref, across_ref, wa_ref, wl_ref, picked_ref, pick_ref, trace_ref, flux_ref, emit)
 
 
-def call(kernel, name, args, outs, scratch, flops):
+def call(kernel, name, args, outs, scratch, flops, far=(), vmem_bytes=20 << 20):
     spec = pl.BlockSpec(memory_space=pltpu.VMEM)
+    hbm = pl.BlockSpec(memory_space=pltpu.HBM)
     size = sum(4 * math.prod(a.shape) for a in list(args) + list(outs))
     return pl.pallas_call(
         kernel,
         out_shape=[jax.ShapeDtypeStruct(s.shape, s.dtype) for s in outs],
-        in_specs=[spec] * len(args),
+        in_specs=[hbm if i in far else spec for i in range(len(args))],
         out_specs=[spec] * len(outs),
         scratch_shapes=scratch,
         cost_estimate=pl.CostEstimate(flops=flops, bytes_accessed=size, transcendentals=0),
+        compiler_params=pltpu.CompilerParams(vmem_limit_bytes=vmem_bytes),
         name=name,
-    )(*args)
+    )(*[pltpu.with_memory_space_constraint(a, pltpu.HBM) if i in far else a for i, a in enumerate(args)])
 
 
 def exchange(block, axis, offset):
@@ -408,11 +430,10 @@
     plus = jnp.transpose(flux_plus, (1, 2, 0, 3))
     project = jnp.transpose(project, (1, 0, 2))
     lift = jnp.transpose(lift, (2, 0, 1))
-    cluster = cluster.reshape(1, n)
 
     field = jax.ShapeDtypeStruct((quantities, rows, n), f32)
     traces = jax.ShapeDtypeStruct((quantities, tall, n), f32)
-    sends = jax.ShapeDtypeStruct((DIRS, quantities, rows, width), f32)
+    sends = (jax.ShapeDtypeStruct((quantities, rows, width), f32),) * DIRS
     series_w = pltpu.VMEM((9 * rows, 9 * rows), bf16)
     v_field = pltpu.VMEM((quantities, rows, n), f32)
     t_field = pltpu.VMEM((3 * quantities, rows, n), f32)
@@ -421,26 +442,30 @@
     lift_w = pltpu.VMEM((2 * rows, 6 * tall), bf16)
     picked = pltpu.VMEM((faces, 2 * quantities * rows, n), f32)
 
-    first, late, out = call(
+    first, late, *out = call(
         functools.partial(predict_kernel, axes), "predict", (dofs, star, stiffness, send_list),
-        (field, field, sends), [series_w, v_field, t_field], 10_000_000)
+        (field, field, *sends),
+        [series_w, v_field, t_field] + [pltpu.VMEM(a.shape, a.dtype) for a in (stiffness, dofs, star, send_list)]
+        + [pltpu.SemaphoreType.DMA((4,))], 10_000_000, far=(0, 1, 2, 3))
 
     def own(buffer, name):
         return call(
             own_kernel, name, (buffer, star, minus, stiffness, project, neighbour, neighbour_face, face_type),
             (field, traces, traces),
             [pltpu.VMEM((9 * rows + 3 * tall, 9 * rows), bf16), across_w, t_trace, t_field, picked,
-             pltpu.VMEM((n, n), bf16)], 10_000_000)
+             pltpu.VMEM((n, n), bf16), pltpu.VMEM(minus.shape, f32), pltpu.SemaphoreType.DMA(())],
+            10_000_000, far=(2,))
 
     ghost_scratch = [across_w, lift_w, picked, pltpu.VMEM((DIRS * LANES, n), bf16), t_trace, t_trace]
-    got = swap([out[e] for e in range(DIRS)])
+    got = swap(out)
     part, g, across = own(first, "own_first")
-    midway, second, out = call(
+    midway, second, *out = call(
         functools.partial(middle_kernel, axes), "middle",
         (*got, plus, project, lift, neighbour, neighbour_face, face_type, part, g, across, dofs, star, stiffness,
          cluster, late, send_list),
-        (field, field, sends), ghost_scratch + [series_w, v_field, t_field], 10_000_000)
-    got = swap([out[e] for e in range(DIRS)])
+        (field, field, *sends), ghost_scratch + [series_w, v_field, t_field, pltpu.VMEM((n,), jnp.int32), pltpu.SemaphoreType.DMA(())],
+        10_000_000, far=(16,))
+    got = swap(out)
     part, g, across = own(second, "own_second")
     (result,) = call(
         functools.partial(finish_kernel, axes), "finish",

time: 56 us -> 41.9 us (0.75)
  the two profiles are of different devices: /device:TPU:0 before, /device:TPU:13 now
where the time goes in v1:
time: 41.9 us; the launch traced here: 41.7 us
  Pallas kernels  24.1 us (58%)
  starting transfers between devices  16.5 us (39%)
  local copies, waits for them, and re-layouts  0.69 us (2%)
    pallas_call x5, Pallas kernels, call(): pl.pallas_call(kernel, out_shape=[jax.ShapeDtypeStruct(s.shape, s.dtype)...  24.1 us
    ppermute x8, starting transfers between devices, exchange(): return lax.ppermute(block, axis, route)  16.5 us
  transfers between devices with their start and end apart: 8, of which 0 were waited for; matrix products, arithmetic and copies ran while one was open for 0% of the time, Pallas kernels for 18%

profile of v1, /device:TPU:13, one launch (start us, length us, event | category | flops | bytes accessed | tf_op | source)
XLA Modules:
  0.0 41.7 jit_solution(10472891849023264580)
XLA Ops:
  0.0 0.0 copy-start.7
  0.0 5.5 %predict.1 = (f32[9,24,384]{2,1,0:T(8,128)S(1)}, f32[9,24,384]{2,1,0:T(8,128)S(1)}, f32[9,24,96]{2,1,0:T(8,128)S(1)}, f32[9,24,96]{2,1,0:T(8,128)S(1)}, f32[9,24...) custom-call(f32[9,20,384]{2,1,0:T(8,128)} %dofs_ref.1, f32[9,9,3,384]{3,2,1,0:T(4,128)} %bitcast.5, f32[3,20,20]{2,1,0:T(8,128)} %stiff_ref.5, ...), custom_call_target="tpu_custom_call" | custom-call | flops 10000000 | bytes 1651392 | tf_op jit(solution)/shard_map/predict/pallas_call | solution.py:391
  5.5 0.0 copy-start.6
  5.5 0.0 copy-start.5
  5.5 0.3 collective-permute-start
  5.9 4.1 %collective-permute-start.1 = (f32[9,24,96]{2,1,0:T(8,128)S(1)}, f32[9,24,96]{2,1,0:T(8,128)S(1)}, u32[]{:S(2)}, u32[]{:S(2)}) collective-permute-start(f32[9,24,96]{2,1,0:T(8,128)S(1)} %get-tuple-element.24), channel_id=1, source_target_pairs={{4,8},{8,4},{12,16},{16,12},{20,24},{24,20},{5,9},{9,5},{13,17},{1... | collective-permute-start | bytes 248840 | tf_op jit(solution)/shard_map/ppermute | solution.py:408
  10.0 1.3 %collective-permute-start.2 = (f32[9,24,96]{2,1,0:T(8,128)S(1)}, f32[9,24,96]{2,1,0:T(8,128)S(1)}, u32[]{:S(2)}, u32[]{:S(2)}) collective-permute-start(f32[9,24,96]{2,1,0:T(8,128)S(1)} %get-tuple-element.25), channel_id=1, source_target_pairs={{0,1},{1,0},{2,3},{3,2},{4,5},{5,4},{6,7},{7,6},{8,9},{9,8},{10,11... | collective-permute-start | bytes 248840 | tf_op jit(solution)/shard_map/ppermute | solution.py:408
  11.3 3.0 %collective-permute-start.3 = (f32[9,24,96]{2,1,0:T(8,128)S(1)}, f32[9,24,96]{2,1,0:T(8,128)S(1)}, u32[]{:S(2)}, u32[]{:S(2)}) collective-permute-start(f32[9,24,96]{2,1,0:T(8,128)S(1)} %get-tuple-element.26), channel_id=1, source_target_pairs={{1,2},{2,1},{5,6},{6,5},{9,10},{10,9},{13,14},{14,13},{17,18},{18,... | collective-permute-start | bytes 248840 | tf_op jit(solution)/shard_map/ppermute | solution.py:408
  14.3 0.0 copy-done
  14.3 0.0 copy-done.3
  14.3 0.0 copy-done.4
  14.4 0.0 copy-start.1
  14.4 0.0 copy-start.2
  14.4 0.0 copy-start.8
  14.4 3.8 %own_first.1 = (f32[9,24,384]{2,1,0:T(8,128)S(1)}, f32[9,40,384]{2,1,0:T(8,128)S(1)}, f32[9,40,384]{2,1,0:T(8,128)S(1)}) custom-call(f32[9,24,384]{2,1,0:T(8,128)S(1)} %get-tuple-element.27.own_ref, f32[9,9,3,384]{3,2,1,0:T(4,128)S(1)} %bitcast.6, f32[9,9,4,384]{3,2,1,0:T(4,128)} %bitcast.17, f32[3,20,20]{2,1,0:T(8,128)S(1)} %copy-done.3, ...), custom_call_target="tpu_custom_call" | custom-call | flops 10000000 | bytes 2666816 | tf_op jit(solution)/shard_map/own_first/pallas_call | solution.py:391
  18.3 0.0 collective-permute-done.got0
  18.3 0.0 collective-permute-done.1.got1
  18.3 0.0 collective-permute-done.2.got2
  18.3 0.0 collective-permute-done.3.got3
  18.3 0.0 copy-start.9
  18.3 0.6 %copy-done.9 = s32[4,96]{1,0:T(4,128)S(1)} copy-done((s32[4,96]{1,0:T(4,128)S(1)}, s32[4,96]{1,0:T(4,128)}, u32[]{:S(2)}) %copy-start.9) | copy-done | bytes 1560
  19.0 7.3 %middle.1 = (f32[9,24,384]{2,1,0:T(8,128)S(1)}, f32[9,24,384]{2,1,0:T(8,128)S(1)}, f32[9,24,96]{2,1,0:T(8,128)S(1)}, f32[9,24,96]{2,1,0:T(8,128)S(1)}, f32[9,24,...) custom-call(f32[9,24,96]{2,1,0:T(8,128)S(1)} %collective-permute-done.got0, f32[9,24,96]{2,1,0:T(8,128)S(1)} %collective-permute-done.1.got1, ...), custom_call_target="tpu_custom_call" | custom-call | flops 10000000 | bytes 4276672 | tf_op jit(solution)/shard_map/middle/pallas_call | solution.py:391
  26.2 0.1 collective-permute-start.4
  26.3 4.4 %collective-permute-start.5 = (f32[9,24,96]{2,1,0:T(8,128)S(1)}, f32[9,24,96]{2,1,0:T(8,128)S(1)}, u32[]{:S(2)}, u32[]{:S(2)}) collective-permute-start(f32[9,24,96]{2,1,0:T(8,128)S(1)} %get-tuple-element.33), channel_id=1, source_target_pairs={{4,8},{8,4},{12,16},{16,12},{20,24},{24,20},{5,9},{9,5},{13,17},{1... | collective-permute-start | bytes 248840 | tf_op jit(solution)/shard_map/ppermute | solution.py:408
  30.7 0.1 collective-permute-start.6
  30.8 3.3 %collective-permute-start.7 = (f32[9,24,96]{2,1,0:T(8,128)S(1)}, f32[9,24,96]{2,1,0:T(8,128)S(1)}, u32[]{:S(2)}, u32[]{:S(2)}) collective-permute-start(f32[9,24,96]{2,1,0:T(8,128)S(1)} %get-tuple-element.35), channel_id=1, source_target_pairs={{1,2},{2,1},{5,6},{6,5},{9,10},{10,9},{13,14},{14,13},{17,18},{18,... | collective-permute-start | bytes 248840 | tf_op jit(solution)/shard_map/ppermute | solution.py:408
  34.1 3.8 %own_second.1 = (f32[9,24,384]{2,1,0:T(8,128)S(1)}, f32[9,40,384]{2,1,0:T(8,128)S(1)}, f32[9,40,384]{2,1,0:T(8,128)S(1)}) custom-call(f32[9,24,384]{2,1,0:T(8,128)S(1)} %get-tuple-element.36.own_ref, f32[9,9,3,384]{3,2,1,0:T(4,128)S(1)} %bitcast.8, f32[9,9,4,384]{3,2,1,0:T(4,128)} %bitcast.18, f32[3,20,20]{2,1,0:T(8,128)S(1)} %copy-done.3, ...), custom_call_target="tpu_custom_call" | custom-call | flops 10000000 | bytes 2666816 | tf_op jit(solution)/shard_map/own_second/pallas_call | solution.py:391
  37.9 0.0 collective-permute-done.4.got0
  37.9 0.0 collective-permute-done.5.got1
  37.9 0.0 collective-permute-done.6.got2
  37.9 0.0 collective-permute-done.7.got3
  37.9 3.7 %finish.1 = f32[9,20,384]{2,1,0:T(8,128)} custom-call(f32[9,24,96]{2,1,0:T(8,128)S(1)} %collective-permute-done.4.got0, f32[9,24,96]{2,1,0:T(8,128)S(1)} %collective-permute-done.5.got1, f32[9,24,96]{2,1,0:T(8,128)S(1)} %collective-permute-done.6.got2, f32[9,24,96]{2,1,0:T(8,128)S(1)} %collective-permute-done.7.got3, f32[9,9,4,384]{3,2,1,0:T(4,128)S(1)} %bitcast.10, ...), custom_call_target="tpu_custom_call" | custom-call | flops 10000000 | bytes 2900224 | tf_op jit(solution)/shard_map/finish/pallas_call | solution.py:391
  (9 shorter events, 0.0 us)
Async XLA Ops:
  0.0 14.3 %copy-start = (f32[3,9,9,384]{3,0,2,1:T(4,128)S(1)}, f32[3,9,9,384]{3,0,2,1:T(4,128)}, u32[]{:S(2)}) copy-start(f32[3,9,9,384]{3,0,2,1:T(4,128)} %param.13) | copy-start | bytes 1119748
  0.0 14.3 %copy-start.3 = (f32[3,20,20]{2,1,0:T(8,128)S(1)}, f32[3,20,20]{2,1,0:T(8,128)}, u32[]{:S(2)}) copy-start(f32[3,20,20]{2,1,0:T(8,128)} %stiff_ref.5) | copy-start | bytes 14404
  0.0 14.3 %copy-start.4 = (f32[4,10,20]{2,0,1:T(4,128)S(1)}, f32[4,10,20]{2,0,1:T(4,128)}, u32[]{:S(2)}) copy-start(f32[4,10,20]{2,0,1:T(4,128)} %param.17) | copy-start | bytes 9604
  0.0 14.3 %copy-start.7 = (s32[4,384]{1,0:T(4,128)S(1)}, s32[4,384]{1,0:T(4,128)}, u32[]{:S(2)}) copy-start(s32[4,384]{1,0:T(4,128)} %type_ref.7) | copy-start | bytes 18436
  5.5 8.8 %copy-start.6 = (s32[4,384]{1,0:T(4,128)S(1)}, s32[4,384]{1,0:T(4,128)}, u32[]{:S(2)}) copy-start(s32[4,384]{1,0:T(4,128)} %face_ref.7) | copy-start | bytes 18436
  5.5 8.8 %copy-start.5 = (s32[4,384]{1,0:T(4,128)S(1)}, s32[4,384]{1,0:T(4,128)}, u32[]{:S(2)}) copy-start(s32[4,384]{1,0:T(4,128)} %near_ref.7) | copy-start | bytes 18436
  5.5 12.7 %collective-permute-start = (f32[9,24,96]{2,1,0:T(8,128)S(1)}, f32[9,24,96]{2,1,0:T(8,128)S(1)}, u32[]{:S(2)}, u32[]{:S(2)}) collective-permute-start(f32[9,24,96]{2,1,0:T(8,128)S(1)} %get-tuple-element.23), channel_id=1, source_target_pairs={{0,4},{4,0},{8,12},{12,8},{16,20},{20,16},{24,28},{28,24},{1,5},{5... | collective-permute-start | bytes 248840 | tf_op jit(solution)/shard_map/ppermute | solution.py:408
  5.9 12.4 %collective-permute-start.1 = (f32[9,24,96]{2,1,0:T(8,128)S(1)}, f32[9,24,96]{2,1,0:T(8,128)S(1)}, u32[]{:S(2)}, u32[]{:S(2)}) collective-permute-start(f32[9,24,96]{2,1,0:T(8,128)S(1)} %get-tuple-element.24), channel_id=1, source_target_pairs={{4,8},{8,4},{12,16},{16,12},{20,24},{24,20},{5,9},{9,5},{13,17},{1... | collective-permute-start | bytes 248840 | tf_op jit(solution)/shard_map/ppermute | solution.py:408
  10.0 8.3 %collective-permute-start.2 = (f32[9,24,96]{2,1,0:T(8,128)S(1)}, f32[9,24,96]{2,1,0:T(8,128)S(1)}, u32[]{:S(2)}, u32[]{:S(2)}) collective-permute-start(f32[9,24,96]{2,1,0:T(8,128)S(1)} %get-tuple-element.25), channel_id=1, source_target_pairs={{0,1},{1,0},{2,3},{3,2},{4,5},{5,4},{6,7},{7,6},{8,9},{9,8},{10,11... | collective-permute-start | bytes 248840 | tf_op jit(solution)/shard_map/ppermute | solution.py:408
  11.3 7.0 %collective-permute-start.3 = (f32[9,24,96]{2,1,0:T(8,128)S(1)}, f32[9,24,96]{2,1,0:T(8,128)S(1)}, u32[]{:S(2)}, u32[]{:S(2)}) collective-permute-start(f32[9,24,96]{2,1,0:T(8,128)S(1)} %get-tuple-element.26), channel_id=1, source_target_pairs={{1,2},{2,1},{5,6},{6,5},{9,10},{10,9},{13,14},{14,13},{17,18},{18,... | collective-permute-start | bytes 248840 | tf_op jit(solution)/shard_map/ppermute | solution.py:408
  14.4 3.9 %copy-start.1 = (f32[4,9,9,384]{3,0,2,1:T(4,128)S(1)}, f32[4,9,9,384]{3,0,2,1:T(4,128)}, u32[]{:S(2)}) copy-start(f32[4,9,9,384]{3,0,2,1:T(4,128)} %param.15) | copy-start | bytes 1492996
  14.4 3.9 %copy-start.2 = (f32[9,20,384]{2,1,0:T(8,128)S(1)}, f32[9,20,384]{2,1,0:T(8,128)}, u32[]{:S(2)}) copy-start(f32[9,20,384]{2,1,0:T(8,128)} %dofs_ref.1) | copy-start | bytes 829444
  14.4 3.9 %copy-start.8 = (f32[4,20,10]{1,0,2:T(4,128)S(1)}, f32[4,20,10]{1,0,2:T(4,128)}, u32[]{:S(2)}) copy-start(f32[4,20,10]{1,0,2:T(4,128)} %param.18) | copy-start | bytes 9604
  18.3 0.7 %copy-start.9 = (s32[4,96]{1,0:T(4,128)S(1)}, s32[4,96]{1,0:T(4,128)}, u32[]{:S(2)}) copy-start(s32[4,96]{1,0:T(4,128)} %lists_ref.1) | copy-start | bytes 4612
  26.2 11.7 %collective-permute-start.4 = (f32[9,24,96]{2,1,0:T(8,128)S(1)}, f32[9,24,96]{2,1,0:T(8,128)S(1)}, u32[]{:S(2)}, u32[]{:S(2)}) collective-permute-start(f32[9,24,96]{2,1,0:T(8,128)S(1)} %get-tuple-element.32), channel_id=1, source_target_pairs={{0,4},{4,0},{8,12},{12,8},{16,20},{20,16},{24,28},{28,24},{1,5},{5... | collective-permute-start | bytes 248840 | tf_op jit(solution)/shard_map/ppermute | solution.py:408
  26.3 11.6 %collective-permute-start.5 = (f32[9,24,96]{2,1,0:T(8,128)S(1)}, f32[9,24,96]{2,1,0:T(8,128)S(1)}, u32[]{:S(2)}, u32[]{:S(2)}) collective-permute-start(f32[9,24,96]{2,1,0:T(8,128)S(1)} %get-tuple-element.33), channel_id=1, source_target_pairs={{4,8},{8,4},{12,16},{16,12},{20,24},{24,20},{5,9},{9,5},{13,17},{1... | collective-permute-start | bytes 248840 | tf_op jit(solution)/shard_map/ppermute | solution.py:408
  30.7 7.2 %collective-permute-start.6 = (f32[9,24,96]{2,1,0:T(8,128)S(1)}, f32[9,24,96]{2,1,0:T(8,128)S(1)}, u32[]{:S(2)}, u32[]{:S(2)}) collective-permute-start(f32[9,24,96]{2,1,0:T(8,128)S(1)} %get-tuple-element.34), channel_id=1, source_target_pairs={{0,1},{1,0},{2,3},{3,2},{4,5},{5,4},{6,7},{7,6},{8,9},{9,8},{10,11... | collective-permute-start | bytes 248840 | tf_op jit(solution)/shard_map/ppermute | solution.py:408
  30.8 7.1 %collective-permute-start.7 = (f32[9,24,96]{2,1,0:T(8,128)S(1)}, f32[9,24,96]{2,1,0:T(8,128)S(1)}, u32[]{:S(2)}, u32[]{:S(2)}) collective-permute-start(f32[9,24,96]{2,1,0:T(8,128)S(1)} %get-tuple-element.35), channel_id=1, source_target_pairs={{1,2},{2,1},{5,6},{6,5},{9,10},{10,9},{13,14},{14,13},{17,18},{18,... | collective-permute-start | bytes 248840 | tf_op jit(solution)/shard_map/ppermute | solution.py:408

commit v2 on v1

--- a/solution.py
+++ b/solution.py
@@ -101,13 +101,14 @@
                 t_ref[c * quantities + 3 * g + i, :, lane] = t[start : start + rows]
 
 
-def series(w_ref, v_ref, t_ref, star_ref, sums):
+def series(w_ref, v_ref, t_ref, star_ref, sums, ready=lambda: None):
     quantities, _, n = v_ref.shape
     tiles = n // LANES
     for ref, weights in sums:
         for q in range(quantities):
             ref[q] = weights[0] * v_ref[q]
     stiff_products(w_ref, v_ref, t_ref, pl.ds(0, n))
+    ready()
     for m in range(1, 4):
 
         def tile(index, carry, m=m):
@@ -132,6 +133,7 @@
     both = jnp.concatenate([high, low], axis=0)
     count = lists_ref.shape[1]
     wanted = lists_ref[...]
+    picks = []
     for e in range(DIRS):
         axis = e // 2
         even, odd = (1, 0) if e % 2 == 0 else (0, 1)
@@ -140,33 +142,44 @@
             wanted[2 * axis + even : 2 * axis + even + 1],
             wanted[2 * axis + odd : 2 * axis + odd + 1],
         )
-        pick = (iota((n, count), 0) == row).astype(bf16)
-        got = jnp.dot(both, pick, preferred_element_type=f32)
-        total = got[: quantities * rows] + got[quantities * rows :]
+        row = jnp.concatenate([row, jnp.full((1, LANES - count), -1, jnp.int32)], axis=1)
+        picks.append((iota((n, LANES), 0) == row).astype(bf16))
+    got = jnp.dot(both, jnp.concatenate(picks, axis=1), preferred_element_type=f32)
+    total = got[: quantities * rows] + got[quantities * rows :]
+    for e in range(DIRS):
         for q in range(quantities):
-            out_refs[e][q] = total[q * rows : (q + 1) * rows]
+            out_refs[e][q] = total[q * rows : (q + 1) * rows, e * LANES : e * LANES + count]
 
 
 def parities(axes):
     return [lax.rem(lax.axis_index(axis), 2) for axis in axes]
 
 
-def predict_kernel(axes, dofs_in, star_in, stiff_in, lists_in, first_ref, late_ref, s0, s1, s2, s3,
-                   w_ref, v_ref, t_ref, stiff_ref, dofs_ref, star_ref, lists_ref, sems):
+def predict_kernel(axes, stiff_in, project_in, lift_in, dofs_in, star_in, lists_in,
+                   first_ref, late_ref, s0, s1, s2, s3, w_ref, wo_ref, wa_ref, wl_ref,
+                   v_ref, t_ref, stiff_ref, project_ref, lift_ref, dofs_ref, star_ref, lists_ref, sems):
     h = step_length
     rows = first_ref.shape[1]
-    pairs = [(stiff_in, stiff_ref), (dofs_in, dofs_ref), (star_in, star_ref), (lists_in, lists_ref)]
+    pairs = [(stiff_in, stiff_ref), (project_in, project_ref), (lift_in, lift_ref),
+             (dofs_in, dofs_ref), (star_in, star_ref), (lists_in, lists_ref)]
     copies = [pltpu.make_async_copy(src, dst, sems.at[i]) for i, (src, dst) in enumerate(pairs)]
     for copy in copies:
         copy.start()
-    copies[0].wait()
+    for copy in copies[:3]:
+        copy.wait()
+    faces_basis = project_ref.shape[0]
+    flat = jnp.concatenate([project_ref[b] for b in range(faces_basis)], axis=0)
     w_ref[...] = series_weights(stiff_ref, rows, False)
-    for copy in copies[1:]:
-        copy.wait()
+    wo_ref[: 9 * rows] = series_weights(stiff_ref, rows, True)
+    wo_ref[9 * rows :] = jnp.concatenate(block_weights(flat, rows, 3, False), axis=0).astype(bf16)
+    wa_ref[...] = across_weights(project_ref)
+    wl_ref[...] = lift_weights(lift_ref, rows)
+    copies[3].wait()
     for q in range(dofs_ref.shape[0]):
         v_ref[q] = pad_rows(dofs_ref[q], rows)
     sums = [(first_ref, weights_of(0.0, h)), (late_ref, weights_of(h, 2 * h))]
-    series(w_ref, v_ref, t_ref, star_ref, sums)
+    series(w_ref, v_ref, t_ref, star_ref, sums, copies[4].wait)
+    copies[5].wait()
     pack_sends(first_ref, lists_ref, [s0, s1, s2, s3], parities(axes))
 
 
@@ -223,14 +236,17 @@
     tall = w_ref.shape[0] // faces
     wide = jnp.concatenate([source] * (tall // faces), axis=0)
     tests = [wide == g for g in range(faces - 1)]
-    for q in range(quantities):
-        z = jnp.dot(
-            w_ref[...], across_operand(picked, q, rows, height), preferred_element_type=f32
-        )
-        value = z[(faces - 1) * tall :]
-        for g in reversed(range(faces - 1)):
-            value = jnp.where(tests[g], z[g * tall : (g + 1) * tall], value)
-        store(q, value)
+    n = source.shape[1]
+    for first in range(0, quantities, 2):
+        group = range(first, min(first + 2, quantities))
+        x = jnp.concatenate([across_operand(picked, q, rows, height) for q in group], axis=1)
+        z = jnp.dot(w_ref[...], x, preferred_element_type=f32)
+        for i, q in enumerate(group):
+            mine = z[:, i * n : (i + 1) * n]
+            value = mine[(faces - 1) * tall :]
+            for g in reversed(range(faces - 1)):
+                value = jnp.where(tests[g], mine[g * tall : (g + 1) * tall], value)
+            store(q, value)
 
 
 def flux_mix(flux_ref, trace_ref, lane, start):
@@ -246,39 +262,39 @@
     return acc
 
 
-def own_kernel(own_ref, star_ref, minus_in, stiff_ref, project_ref, near_ref, face_ref, type_ref,
-               part_ref, g_ref, across_ref, w_ref, wa_ref, trace_ref, t_ref, picked_ref, pick_ref, minus_ref, sem):
+def gather(operand, index, picked_ref):
+    faces, n = index.shape
+    picks = [(iota((operand.shape[1], n), 0) == index[f : f + 1]).astype(bf16) for f in range(faces)]
+    picked_ref[...] = jnp.dot(operand, jnp.concatenate(picks, axis=1), preferred_element_type=f32)
+    return [picked_ref.at[:, f * n : (f + 1) * n] for f in range(faces)]
+
+
+def own_kernel(own_ref, star_ref, minus_in, w_ref, wa_ref, near_ref, face_ref, type_ref,
+               part_ref, g_ref, across_ref, trace_ref, t_ref, picked_ref, minus_ref, sem):
     minus_copy = pltpu.make_async_copy(minus_in, minus_ref, sem)
     minus_copy.start()
     quantities, rows, n = own_ref.shape
-    faces_basis, faces, count = project_ref.shape
-    tall = faces_basis * faces
-    flat = jnp.concatenate([project_ref[b] for b in range(faces_basis)], axis=0)
-    w_ref[: 9 * rows] = series_weights(stiff_ref, rows, True)
-    w_ref[9 * rows :] = jnp.concatenate(block_weights(flat, rows, 3, False), axis=0).astype(bf16)
-    wa_ref[...] = across_weights(project_ref)
-    for g in range(quantities // 3):
-        x = triple(stacked(own_ref, 3 * g, 3))
-        t = jnp.dot(w_ref[...], x, preferred_element_type=f32)
+    tall = trace_ref.shape[1]
+    groups = quantities // 3
+    x = jnp.concatenate([triple(stacked(own_ref, 3 * g, 3)) for g in range(groups)], axis=1)
+    t = jnp.dot(w_ref[...], x, preferred_element_type=f32)
+    for g in range(groups):
         for c in range(3):
             for i in range(3):
                 start = (3 * c + i) * rows
-                t_ref[c * quantities + 3 * g + i] = t[start : start + rows]
+                t_ref[c * quantities + 3 * g + i] = t[start : start + rows, g * n : (g + 1) * n]
         for i in range(3):
             start = 9 * rows + i * tall
-            trace_ref[3 * g + i] = t[start : start + tall]
+            trace_ref[3 * g + i] = t[start : start + tall, g * n : (g + 1) * n]
 
     index, source = effective(type_ref, near_ref, face_ref)
     high, low = split(stacked(own_ref, 0, quantities))
-    both = jnp.concatenate([high, low], axis=0)
-    for f in range(faces):
-        pick_ref[...] = (iota((n, n), 0) == index[f : f + 1]).astype(bf16)
-        picked_ref[f] = jnp.dot(both, pick_ref[...], preferred_element_type=f32)
+    picked = gather(jnp.concatenate([high, low], axis=0), index, picked_ref)
 
     def keep(q, value):
         across_ref[q] = value
 
-    across_traces(wa_ref, [picked_ref.at[f] for f in range(faces)], source, quantities, rows, keep)
+    across_traces(wa_ref, picked, source, quantities, rows, keep)
 
     minus_copy.wait()
 
@@ -300,13 +316,10 @@
     return jnp.concatenate([pad_rows(block, rows) for block in blocks], axis=0).astype(bf16)
 
 
-def ghost_part(axes, got_refs, plus_ref, project_ref, lift_ref, near_ref, face_ref, type_ref,
-               part_ref, g_ref, across_ref, wa_ref, wl_ref, picked_ref, pick_ref, trace_ref, flux_ref, emit):
+def ghost_part(axes, got_refs, plus_ref, wa_ref, wl_ref, near_ref, face_ref, type_ref,
+               part_ref, g_ref, across_ref, picked_ref, trace_ref, flux_ref, emit):
     quantities, rows, n = part_ref.shape
-    faces = project_ref.shape[1]
     count = got_refs[0].shape[2]
-    wa_ref[...] = across_weights(project_ref)
-    wl_ref[...] = lift_weights(lift_ref, rows)
     index, source = effective(type_ref, near_ref, face_ref)
     parity = parities(axes)
     ghost = index - n
@@ -320,15 +333,12 @@
         both = jnp.concatenate([high, low], axis=0)
         empty = jnp.zeros((both.shape[0], LANES - count), bf16)
         operands.append(jnp.concatenate([both, empty], axis=1))
-    operand = jnp.concatenate(operands, axis=1)
-    for f in range(faces):
-        pick_ref[...] = (iota((DIRS * LANES, n), 0) == column[f : f + 1]).astype(bf16)
-        picked_ref[f] = jnp.dot(operand, pick_ref[...], preferred_element_type=f32)
+    picked = gather(jnp.concatenate(operands, axis=1), column, picked_ref)
 
     def keep(q, value):
         trace_ref[q] = across_ref[q] + value
 
-    across_traces(wa_ref, [picked_ref.at[f] for f in range(faces)], source, quantities, rows, keep)
+    across_traces(wa_ref, picked, source, quantities, rows, keep)
 
     def tile(lane):
         acc = flux_mix(plus_ref, trace_ref, lane, [g_ref[p, :, lane] for p in range(quantities)])
@@ -336,23 +346,25 @@
             flux_ref[p, :, lane] = acc[p]
 
     lane_tiles(n, tile)
-    for pair in range(0, quantities, 2):
-        two = pair + 1 < quantities
-        x = jnp.concatenate(
-            [flux_ref[pair], flux_ref[pair + 1] if two else jnp.zeros(flux_ref.shape[1:], f32)], axis=0
-        )
-        lifted = jnp.dot(wl_ref[...], triple(x), preferred_element_type=f32)
-        emit(pair, part_ref[pair] - lifted[:rows])
-        if two:
-            emit(pair + 1, part_ref[pair + 1] - lifted[rows:])
-
-
-def middle_kernel(axes, got0, got1, got2, got3, plus_ref, project_ref, lift_ref, near_ref, face_ref, type_ref,
-                  part_ref, g_ref, across_ref, dofs_ref, star_ref, stiff_ref, cluster_in, late_ref, lists_ref,
+    pairs = range(0, quantities, 2)
+    operands = []
+    for pair in pairs:
+        other = flux_ref[pair + 1] if pair + 1 < quantities else jnp.zeros(flux_ref.shape[1:], f32)
+        operands.append(triple(jnp.concatenate([flux_ref[pair], other], axis=0)))
+    lifted = jnp.dot(wl_ref[...], jnp.concatenate(operands, axis=1), preferred_element_type=f32)
+    for q in range(quantities):
+        row, column = (q % 2) * rows, (q // 2) * n
+        emit(q, part_ref[q] - lifted[row : row + rows, column : column + n])
+
+
+def middle_kernel(axes, got0, got1, got2, got3, plus_ref, wa_ref, wl_ref, near_ref, face_ref, type_ref,
+                  part_ref, g_ref, across_ref, dofs_ref, star_ref, w_ref, cluster_in, late_ref, lists_in,
                   midway_ref, second_ref, s0, s1, s2, s3,
-                  wa_ref, wl_ref, picked_ref, pick_ref, trace_ref, flux_ref, w_ref, v_ref, t_ref, cluster_ref, sem):
-    cluster_copy = pltpu.make_async_copy(cluster_in, cluster_ref, sem)
-    cluster_copy.start()
+                  picked_ref, trace_ref, flux_ref, v_ref, t_ref, cluster_ref, lists_ref, sems):
+    copies = [pltpu.make_async_copy(cluster_in, cluster_ref, sems.at[0]),
+              pltpu.make_async_copy(lists_in, lists_ref, sems.at[1])]
+    for copy in copies:
+        copy.start()
     rows = part_ref.shape[1]
     quantities = part_ref.shape[0]
 
@@ -361,27 +373,26 @@
         midway_ref[q] = value
         v_ref[q] = value
 
-    ghost_part(axes, [got0, got1, got2, got3], plus_ref, project_ref, lift_ref, near_ref, face_ref, type_ref,
-               part_ref, g_ref, across_ref, wa_ref, wl_ref, picked_ref, pick_ref, trace_ref, flux_ref, emit)
-    w_ref[...] = series_weights(stiff_ref, rows, False)
+    ghost_part(axes, [got0, got1, got2, got3], plus_ref, wa_ref, wl_ref, near_ref, face_ref, type_ref,
+               part_ref, g_ref, across_ref, picked_ref, trace_ref, flux_ref, emit)
     series(w_ref, v_ref, t_ref, star_ref, [(second_ref, weights_of(0.0, step_length))])
-    cluster_copy.wait()
+    for copy in copies:
+        copy.wait()
     fast = cluster_ref[...][None, :] == 0
     for q in range(quantities):
         second_ref[q] = jnp.where(fast, second_ref[q], late_ref[q])
     pack_sends(second_ref, lists_ref, [s0, s1, s2, s3], parities(axes))
 
 
-def finish_kernel(axes, got0, got1, got2, got3, plus_ref, project_ref, lift_ref, near_ref, face_ref, type_ref,
-                  part_ref, g_ref, across_ref, midway_ref, out_ref,
-                  wa_ref, wl_ref, picked_ref, pick_ref, trace_ref, flux_ref):
+def finish_kernel(axes, got0, got1, got2, got3, plus_ref, wa_ref, wl_ref, near_ref, face_ref, type_ref,
+                  part_ref, g_ref, across_ref, midway_ref, out_ref, picked_ref, trace_ref, flux_ref):
     count = out_ref.shape[1]
 
     def emit(q, change):
         out_ref[q] = (midway_ref[q] + change)[:count]
 
-    ghost_part(axes, [got0, got1, got2, got3], plus_ref, project_ref, lift_ref, near_ref, face_ref, type_ref,
-               part_ref, g_ref, across_ref, wa_ref, wl_ref, picked_ref, pick_ref, trace_ref, flux_ref, emit)
+    ghost_part(axes, [got0, got1, got2, got3], plus_ref, wa_ref, wl_ref, near_ref, face_ref, type_ref,
+               part_ref, g_ref, across_ref, picked_ref, trace_ref, flux_ref, emit)
 
 
 def call(kernel, name, args, outs, scratch, flops, far=(), vmem_bytes=20 << 20):
@@ -434,42 +445,47 @@
     field = jax.ShapeDtypeStruct((quantities, rows, n), f32)
     traces = jax.ShapeDtypeStruct((quantities, tall, n), f32)
     sends = (jax.ShapeDtypeStruct((quantities, rows, width), f32),) * DIRS
-    series_w = pltpu.VMEM((9 * rows, 9 * rows), bf16)
+    weights = (
+        jax.ShapeDtypeStruct((9 * rows, 9 * rows), bf16),
+        jax.ShapeDtypeStruct((9 * rows + 3 * tall, 9 * rows), bf16),
+        jax.ShapeDtypeStruct((faces * tall, 3 * faces * count), bf16),
+        jax.ShapeDtypeStruct((2 * rows, 6 * tall), bf16),
+    )
     v_field = pltpu.VMEM((quantities, rows, n), f32)
     t_field = pltpu.VMEM((3 * quantities, rows, n), f32)
     t_trace = pltpu.VMEM((quantities, tall, n), f32)
-    across_w = pltpu.VMEM((faces * tall, 3 * faces * count), bf16)
-    lift_w = pltpu.VMEM((2 * rows, 6 * tall), bf16)
-    picked = pltpu.VMEM((faces, 2 * quantities * rows, n), f32)
-
+    picked = pltpu.VMEM((2 * quantities * rows, faces * n), f32)
+
+    inputs = (stiffness, project, lift, dofs, star, send_list)
     first, late, *out = call(
-        functools.partial(predict_kernel, axes), "predict", (dofs, star, stiffness, send_list),
-        (field, field, *sends),
-        [series_w, v_field, t_field] + [pltpu.VMEM(a.shape, a.dtype) for a in (stiffness, dofs, star, send_list)]
-        + [pltpu.SemaphoreType.DMA((4,))], 10_000_000, far=(0, 1, 2, 3))
+        functools.partial(predict_kernel, axes), "predict", inputs, (field, field, *sends, *weights),
+        [v_field, t_field] + [pltpu.VMEM(a.shape, a.dtype) for a in inputs]
+        + [pltpu.SemaphoreType.DMA((len(inputs),))], 10_000_000, far=range(len(inputs)))
+    out, (w, wo, wa, wl) = out[:DIRS], out[DIRS:]
 
     def own(buffer, name):
         return call(
-            own_kernel, name, (buffer, star, minus, stiffness, project, neighbour, neighbour_face, face_type),
+            own_kernel, name, (buffer, star, minus, wo, wa, neighbour, neighbour_face, face_type),
             (field, traces, traces),
-            [pltpu.VMEM((9 * rows + 3 * tall, 9 * rows), bf16), across_w, t_trace, t_field, picked,
-             pltpu.VMEM((n, n), bf16), pltpu.VMEM(minus.shape, f32), pltpu.SemaphoreType.DMA(())],
+            [t_trace, t_field, picked, pltpu.VMEM(minus.shape, f32), pltpu.SemaphoreType.DMA(())],
             10_000_000, far=(2,))
 
-    ghost_scratch = [across_w, lift_w, picked, pltpu.VMEM((DIRS * LANES, n), bf16), t_trace, t_trace]
+    ghost_scratch = [picked, t_trace, t_trace]
     got = swap(out)
     part, g, across = own(first, "own_first")
     midway, second, *out = call(
         functools.partial(middle_kernel, axes), "middle",
-        (*got, plus, project, lift, neighbour, neighbour_face, face_type, part, g, across, dofs, star, stiffness,
+        (*got, plus, wa, wl, neighbour, neighbour_face, face_type, part, g, across, dofs, star, w,
          cluster, late, send_list),
-        (field, field, *sends), ghost_scratch + [series_w, v_field, t_field, pltpu.VMEM((n,), jnp.int32), pltpu.SemaphoreType.DMA(())],
-        10_000_000, far=(16,))
+        (field, field, *sends),
+        ghost_scratch + [v_field, t_field, pltpu.VMEM((n,), jnp.int32), pltpu.VMEM(send_list.shape, jnp.int32),
+                         pltpu.SemaphoreType.DMA((2,))],
+        10_000_000, far=(16, 18))
     got = swap(out)
     part, g, across = own(second, "own_second")
     (result,) = call(
         functools.partial(finish_kernel, axes), "finish",
-        (*got, plus, project, lift, neighbour, neighbour_face, face_type, part, g, across, midway),
+        (*got, plus, wa, wl, neighbour, neighbour_face, face_type, part, g, across, midway),
         (jax.ShapeDtypeStruct((quantities, count, n), f32),), ghost_scratch, 10_000_000)
     return result
 

time: 41.9 us -> 38 us (0.907)
  Pallas kernels: 24.1 us -> 20.6 us
  local copies, waits for them, and re-layouts: 0.69 us -> 0.03 us
  starting transfers between devices: 16.5 us -> 17 us
    pallas_call x5, Pallas kernels: 24.1 us -> 20.6 us  [call(): pl.pallas_call(kernel, out_shape=[jax.ShapeDtypeStruct(s.shape, s.dtype)...]
    unnamed x20 -> x12, local copies, waits for them, and re-layouts: 0.69 us -> 0.03 us
    ppermute x8, starting transfers between devices: 16.5 us -> 17 us  [exchange(): return lax.ppermute(block, axis, route)]
  transfers between devices with their start and end apart: 8 -> 8, of which waited for: 0 -> 0; matrix products, arithmetic and copies ran while one was open for 0% -> 0% of each run, Pallas kernels for 18% -> 15%
where the time goes in v2:
time: 38 us; the launch traced here: 37.8 us
  Pallas kernels  20.6 us (54%)
  starting transfers between devices  17 us (45%)
    pallas_call x5, Pallas kernels, call(): pl.pallas_call(kernel, out_shape=[jax.ShapeDtypeStruct(s.shape, s.dtype)...  20.6 us
    ppermute x8, starting transfers between devices, exchange(): return lax.ppermute(block, axis, route)  17 us
  transfers between devices with their start and end apart: 8, of which 0 were waited for; matrix products, arithmetic and copies ran while one was open for 0% of the time, Pallas kernels for 15%

profile of v2, /device:TPU:13, one launch (start us, length us, event | category | flops | bytes accessed | tf_op | source)
XLA Modules:
  0.0 37.8 jit_solution(1489109820166749495)
XLA Ops:
  0.0 0.0 copy-start
  0.0 0.0 copy-start.5
  0.0 5.8 %predict.1 = (f32[9,24,384]{2,1,0:T(8,128)S(1)}, f32[9,24,384]{2,1,0:T(8,128)S(1)}, f32[9,24,96]{2,1,0:T(8,128)S(1)}, f32[9,24,96]{2,1,0:T(8,128)S(1)}, f32[9,24...) custom-call(f32[3,20,20]{2,1,0:T(8,128)} %stiff_in.1, ...), custom_call_target="tpu_custom_call" | custom-call | flops 10000000 | bytes 2334400 | tf_op jit(solution)/shard_map/predict/pallas_call | solution.py:402
  5.8 0.3 collective-permute-start
  6.1 0.0 copy-start.4
  6.1 4.3 %collective-permute-start.1 = (f32[9,24,96]{2,1,0:T(8,128)S(1)}, f32[9,24,96]{2,1,0:T(8,128)S(1)}, u32[]{:S(2)}, u32[]{:S(2)}) collective-permute-start(f32[9,24,96]{2,1,0:T(8,128)S(1)} %get-tuple-element.28), channel_id=1, source_target_pairs={{4,8},{8,4},{12,16},{16,12},{20,24},{24,20},{5,9},{9,5},{13,17},{1... | collective-permute-start | bytes 248840 | tf_op jit(solution)/shard_map/ppermute | solution.py:419
  10.4 1.3 %collective-permute-start.2 = (f32[9,24,96]{2,1,0:T(8,128)S(1)}, f32[9,24,96]{2,1,0:T(8,128)S(1)}, u32[]{:S(2)}, u32[]{:S(2)}) collective-permute-start(f32[9,24,96]{2,1,0:T(8,128)S(1)} %get-tuple-element.29), channel_id=1, source_target_pairs={{0,1},{1,0},{2,3},{3,2},{4,5},{5,4},{6,7},{7,6},{8,9},{9,8},{10,11... | collective-permute-start | bytes 248840 | tf_op jit(solution)/shard_map/ppermute | solution.py:419
  11.7 3.0 %collective-permute-start.3 = (f32[9,24,96]{2,1,0:T(8,128)S(1)}, f32[9,24,96]{2,1,0:T(8,128)S(1)}, u32[]{:S(2)}, u32[]{:S(2)}) collective-permute-start(f32[9,24,96]{2,1,0:T(8,128)S(1)} %get-tuple-element.30), channel_id=1, source_target_pairs={{1,2},{2,1},{5,6},{6,5},{9,10},{10,9},{13,14},{14,13},{17,18},{18,... | collective-permute-start | bytes 248840 | tf_op jit(solution)/shard_map/ppermute | solution.py:419
  14.7 0.0 copy-done
  14.7 0.0 copy-done.5
  14.8 0.0 copy-done.4
  14.8 0.0 copy-done.3
  14.8 0.0 copy-start.1
  14.8 0.0 copy-start.2
  14.8 2.9 %own_first.1 = (f32[9,24,384]{2,1,0:T(8,128)S(1)}, f32[9,40,384]{2,1,0:T(8,128)S(1)}, f32[9,40,384]{2,1,0:T(8,128)S(1)}) custom-call(f32[9,24,384]{2,1,0:T(8,128)S(1)} %get-tuple-element.33.own_ref, f32[9,9,3,384]{3,2,1,0:T(4,128)S(1)} %bitcast.6, f32[9,9,4,384]{3,2,1,0:T(4,128)} %bitcast.11, bf16[336,216]{1,0:T(8,128)(2,1)S(1)} %get-tuple-element.34.w_ref, ...), custom_call_target="tpu_custom_call" | custom-call | flops 10000000 | bytes 3102720 | tf_op jit(solution)/shard_map/own_first/pallas_call | solution.py:402
  17.7 0.0 collective-permute-done.got0
  17.7 0.0 collective-permute-done.1.got1
  17.7 0.0 collective-permute-done.2.got2
  17.7 0.0 collective-permute-done.3.got3
  17.8 0.0 copy-done.1
  17.8 0.0 copy-done.2
  17.8 6.1 %middle.1 = (f32[9,24,384]{2,1,0:T(8,128)S(1)}, f32[9,24,384]{2,1,0:T(8,128)S(1)}, f32[9,24,96]{2,1,0:T(8,128)S(1)}, f32[9,24,96]{2,1,0:T(8,128)S(1)}, f32[9,24,...) custom-call(f32[9,24,96]{2,1,0:T(8,128)S(1)} %collective-permute-done.got0, f32[9,24,96]{2,1,0:T(8,128)S(1)} %collective-permute-done.1.got1, ...), custom_call_target="tpu_custom_call" | custom-call | flops 10000000 | bytes 4651776 | tf_op jit(solution)/shard_map/middle/pallas_call | solution.py:402
  23.9 0.1 collective-permute-start.4
  24.0 4.4 %collective-permute-start.5 = (f32[9,24,96]{2,1,0:T(8,128)S(1)}, f32[9,24,96]{2,1,0:T(8,128)S(1)}, u32[]{:S(2)}, u32[]{:S(2)}) collective-permute-start(f32[9,24,96]{2,1,0:T(8,128)S(1)} %get-tuple-element.41), channel_id=1, source_target_pairs={{4,8},{8,4},{12,16},{16,12},{20,24},{24,20},{5,9},{9,5},{13,17},{1... | collective-permute-start | bytes 248840 | tf_op jit(solution)/shard_map/ppermute | solution.py:419
  28.4 0.1 collective-permute-start.6
  28.4 3.6 %collective-permute-start.7 = (f32[9,24,96]{2,1,0:T(8,128)S(1)}, f32[9,24,96]{2,1,0:T(8,128)S(1)}, u32[]{:S(2)}, u32[]{:S(2)}) collective-permute-start(f32[9,24,96]{2,1,0:T(8,128)S(1)} %get-tuple-element.43), channel_id=1, source_target_pairs={{1,2},{2,1},{5,6},{6,5},{9,10},{10,9},{13,14},{14,13},{17,18},{18,... | collective-permute-start | bytes 248840 | tf_op jit(solution)/shard_map/ppermute | solution.py:419
  32.0 2.9 %own_second.1 = (f32[9,24,384]{2,1,0:T(8,128)S(1)}, f32[9,40,384]{2,1,0:T(8,128)S(1)}, f32[9,40,384]{2,1,0:T(8,128)S(1)}) custom-call(f32[9,24,384]{2,1,0:T(8,128)S(1)} %get-tuple-element.44.own_ref, f32[9,9,3,384]{3,2,1,0:T(4,128)S(1)} %bitcast.8, f32[9,9,4,384]{3,2,1,0:T(4,128)} %bitcast.12, bf16[336,216]{1,0:T(8,128)(2,1)S(1)} %get-tuple-element.34.w_ref, ...), custom_call_target="tpu_custom_call" | custom-call | flops 10000000 | bytes 3102720 | tf_op jit(solution)/shard_map/own_second/pallas_call | solution.py:402
  35.0 0.0 collective-permute-done.4.got0
  35.0 0.0 collective-permute-done.5.got1
  35.0 0.0 collective-permute-done.6.got2
  35.0 0.0 collective-permute-done.7.got3
  35.0 2.8 %finish.1 = f32[9,20,384]{2,1,0:T(8,128)} custom-call(f32[9,24,96]{2,1,0:T(8,128)S(1)} %collective-permute-done.4.got0, f32[9,24,96]{2,1,0:T(8,128)S(1)} %collective-permute-done.5.got1, f32[9,24,96]{2,1,0:T(8,128)S(1)} %collective-permute-done.6.got2, f32[9,24,96]{2,1,0:T(8,128)S(1)} %collective-permute-done.7.got3, f32[9,9,4,384]{3,2,1,0:T(4,128)S(1)} %bitcast.10, ...), custom_call_target="tpu_custom_call" | custom-call | flops 10000000 | bytes 3093504 | tf_op jit(solution)/shard_map/finish/pallas_call | solution.py:402
  (1 shorter events, 0.0 us)
Async XLA Ops:
  0.0 14.7 %copy-start = (f32[3,9,9,384]{3,0,2,1:T(4,128)S(1)}, f32[3,9,9,384]{3,0,2,1:T(4,128)}, u32[]{:S(2)}) copy-start(f32[3,9,9,384]{3,0,2,1:T(4,128)} %param.13) | copy-start | bytes 1119748
  0.0 14.7 %copy-start.5 = (s32[4,384]{1,0:T(4,128)S(1)}, s32[4,384]{1,0:T(4,128)}, u32[]{:S(2)}) copy-start(s32[4,384]{1,0:T(4,128)} %type_ref.7) | copy-start | bytes 18436
  5.8 11.9 %collective-permute-start = (f32[9,24,96]{2,1,0:T(8,128)S(1)}, f32[9,24,96]{2,1,0:T(8,128)S(1)}, u32[]{:S(2)}, u32[]{:S(2)}) collective-permute-start(f32[9,24,96]{2,1,0:T(8,128)S(1)} %get-tuple-element.27), channel_id=1, source_target_pairs={{0,4},{4,0},{8,12},{12,8},{16,20},{20,16},{24,28},{28,24},{1,5},{5... | collective-permute-start | bytes 248840 | tf_op jit(solution)/shard_map/ppermute | solution.py:419
  6.1 8.6 %copy-start.4 = (s32[4,384]{1,0:T(4,128)S(1)}, s32[4,384]{1,0:T(4,128)}, u32[]{:S(2)}) copy-start(s32[4,384]{1,0:T(4,128)} %face_ref.7) | copy-start | bytes 18436
  6.1 8.6 %copy-start.3 = (s32[4,384]{1,0:T(4,128)S(1)}, s32[4,384]{1,0:T(4,128)}, u32[]{:S(2)}) copy-start(s32[4,384]{1,0:T(4,128)} %near_ref.7) | copy-start | bytes 18436
  6.1 11.6 %collective-permute-start.1 = (f32[9,24,96]{2,1,0:T(8,128)S(1)}, f32[9,24,96]{2,1,0:T(8,128)S(1)}, u32[]{:S(2)}, u32[]{:S(2)}) collective-permute-start(f32[9,24,96]{2,1,0:T(8,128)S(1)} %get-tuple-element.28), channel_id=1, source_target_pairs={{4,8},{8,4},{12,16},{16,12},{20,24},{24,20},{5,9},{9,5},{13,17},{1... | collective-permute-start | bytes 248840 | tf_op jit(solution)/shard_map/ppermute | solution.py:419
  10.4 7.3 %collective-permute-start.2 = (f32[9,24,96]{2,1,0:T(8,128)S(1)}, f32[9,24,96]{2,1,0:T(8,128)S(1)}, u32[]{:S(2)}, u32[]{:S(2)}) collective-permute-start(f32[9,24,96]{2,1,0:T(8,128)S(1)} %get-tuple-element.29), channel_id=1, source_target_pairs={{0,1},{1,0},{2,3},{3,2},{4,5},{5,4},{6,7},{7,6},{8,9},{9,8},{10,11... | collective-permute-start | bytes 248840 | tf_op jit(solution)/shard_map/ppermute | solution.py:419
  11.7 6.1 %collective-permute-start.3 = (f32[9,24,96]{2,1,0:T(8,128)S(1)}, f32[9,24,96]{2,1,0:T(8,128)S(1)}, u32[]{:S(2)}, u32[]{:S(2)}) collective-permute-start(f32[9,24,96]{2,1,0:T(8,128)S(1)} %get-tuple-element.30), channel_id=1, source_target_pairs={{1,2},{2,1},{5,6},{6,5},{9,10},{10,9},{13,14},{14,13},{17,18},{18,... | collective-permute-start | bytes 248840 | tf_op jit(solution)/shard_map/ppermute | solution.py:419
  14.8 3.0 %copy-start.1 = (f32[4,9,9,384]{3,0,2,1:T(4,128)S(1)}, f32[4,9,9,384]{3,0,2,1:T(4,128)}, u32[]{:S(2)}) copy-start(f32[4,9,9,384]{3,0,2,1:T(4,128)} %param.15) | copy-start | bytes 1492996
  14.8 3.0 %copy-start.2 = (f32[9,20,384]{2,1,0:T(8,128)S(1)}, f32[9,20,384]{2,1,0:T(8,128)}, u32[]{:S(2)}) copy-start(f32[9,20,384]{2,1,0:T(8,128)} %dofs_ref.1) | copy-start | bytes 829444
  23.9 11.1 %collective-permute-start.4 = (f32[9,24,96]{2,1,0:T(8,128)S(1)}, f32[9,24,96]{2,1,0:T(8,128)S(1)}, u32[]{:S(2)}, u32[]{:S(2)}) collective-permute-start(f32[9,24,96]{2,1,0:T(8,128)S(1)} %get-tuple-element.40), channel_id=1, source_target_pairs={{0,4},{4,0},{8,12},{12,8},{16,20},{20,16},{24,28},{28,24},{1,5},{5... | collective-permute-start | bytes 248840 | tf_op jit(solution)/shard_map/ppermute | solution.py:419
  24.0 11.0 %collective-permute-start.5 = (f32[9,24,96]{2,1,0:T(8,128)S(1)}, f32[9,24,96]{2,1,0:T(8,128)S(1)}, u32[]{:S(2)}, u32[]{:S(2)}) collective-permute-start(f32[9,24,96]{2,1,0:T(8,128)S(1)} %get-tuple-element.41), channel_id=1, source_target_pairs={{4,8},{8,4},{12,16},{16,12},{20,24},{24,20},{5,9},{9,5},{13,17},{1... | collective-permute-start | bytes 248840 | tf_op jit(solution)/shard_map/ppermute | solution.py:419
  28.4 6.6 %collective-permute-start.6 = (f32[9,24,96]{2,1,0:T(8,128)S(1)}, f32[9,24,96]{2,1,0:T(8,128)S(1)}, u32[]{:S(2)}, u32[]{:S(2)}) collective-permute-start(f32[9,24,96]{2,1,0:T(8,128)S(1)} %get-tuple-element.42), channel_id=1, source_target_pairs={{0,1},{1,0},{2,3},{3,2},{4,5},{5,4},{6,7},{7,6},{8,9},{9,8},{10,11... | collective-permute-start | bytes 248840 | tf_op jit(solution)/shard_map/ppermute | solution.py:419
  28.4 6.5 %collective-permute-start.7 = (f32[9,24,96]{2,1,0:T(8,128)S(1)}, f32[9,24,96]{2,1,0:T(8,128)S(1)}, u32[]{:S(2)}, u32[]{:S(2)}) collective-permute-start(f32[9,24,96]{2,1,0:T(8,128)S(1)} %get-tuple-element.43), channel_id=1, source_target_pairs={{1,2},{2,1},{5,6},{6,5},{9,10},{10,9},{13,14},{14,13},{17,18},{18,... | collective-permute-start | bytes 248840 | tf_op jit(solution)/shard_map/ppermute | solution.py:419

commit v3 on v2

--- a/solution.py
+++ b/solution.py
@@ -72,10 +72,11 @@
 
 def star_mix(star_ref, t_ref, lane, quantities):
     rows = t_ref.shape[1]
+    within = lane if t_ref.shape[2] > LANES else pl.ds(0, LANES)
     acc = [None] * quantities
     for c in range(3):
         for q in range(quantities):
-            t = t_ref[c * quantities + q, :, lane]
+            t = t_ref[c * quantities + q, :, within]
             for p in range(quantities):
                 term = jnp.broadcast_to(star_ref[p, q, c : c + 1, lane], (rows, LANES)) * t
                 acc[p] = term if acc[p] is None else acc[p] + term
@@ -90,41 +91,49 @@
     lax.fori_loop(0, n // LANES, one, 0)
 
 
-def stiff_products(w_ref, v_ref, t_ref, lane):
+def stiff_products(w_ref, v_ref, t_ref):
     quantities, rows = v_ref.shape[:2]
     for g in range(quantities // 3):
-        x = jnp.concatenate([v_ref[3 * g + i, :, lane] for i in range(3)], axis=0)
-        t = jnp.dot(w_ref[...], triple(x), preferred_element_type=f32)
+        t = jnp.dot(w_ref[...], triple(stacked(v_ref, 3 * g, 3)), preferred_element_type=f32)
         for c in range(3):
             for i in range(3):
                 start = (3 * c + i) * rows
-                t_ref[c * quantities + 3 * g + i, :, lane] = t[start : start + rows]
-
-
-def series(w_ref, v_ref, t_ref, star_ref, sums, ready=lambda: None):
-    quantities, _, n = v_ref.shape
-    tiles = n // LANES
-    for ref, weights in sums:
-        for q in range(quantities):
-            ref[q] = weights[0] * v_ref[q]
-    stiff_products(w_ref, v_ref, t_ref, pl.ds(0, n))
+                t_ref[c * quantities + 3 * g + i] = t[start : start + rows]
+
+
+def series(w_ref, v_refs, t_refs, star_ref, sums, ready=lambda: None):
+    quantities = v_refs[0].shape[0]
+    lanes = [pl.ds(i * LANES, LANES) for i in range(len(v_refs))]
+    for v_ref, t_ref, lane in zip(v_refs, t_refs, lanes):
+        for ref, weights in sums:
+            for q in range(quantities):
+                ref[q, :, lane] = weights[0] * v_ref[q]
+        stiff_products(w_ref, v_ref, t_ref)
     ready()
-    for m in range(1, 4):
-
-        def tile(index, carry, m=m):
-            lane = pl.ds(pl.multiple_of(index * LANES, LANES), LANES)
+
+    def step(degree, last):
+        def weight(weights):
+            if last:
+                return weights[3]
+            return jnp.where(degree == 0, weights[1], weights[2])
+
+        for v_ref, t_ref, lane in zip(v_refs, t_refs, lanes):
             acc = star_mix(star_ref, t_ref, lane, quantities)
             for p in range(quantities):
                 value = -acc[p]
-                if m < 3:
-                    v_ref[p, :, lane] = value
+                if not last:
+                    v_ref[p] = value
                 for ref, weights in sums:
-                    ref[p, :, lane] += weights[m] * value
-            return carry
-
-        lax.fori_loop(0, tiles, tile, 0)
-        if m < 3:
-            stiff_products(w_ref, v_ref, t_ref, pl.ds(0, n))
+                    ref[p, :, lane] += weight(weights) * value
+            if not last:
+                stiff_products(w_ref, v_ref, t_ref)
+
+    def body(degree, carry):
+        step(degree, False)
+        return carry
+
+    lax.fori_loop(0, 2, body, 0)
+    step(2, True)
 
 
 def pack_sends(buffer_ref, lists_ref, out_refs, parity):
@@ -155,14 +164,16 @@
     return [lax.rem(lax.axis_index(axis), 2) for axis in axes]
 
 
-def predict_kernel(axes, stiff_in, project_in, lift_in, dofs_in, star_in, lists_in,
-                   first_ref, late_ref, s0, s1, s2, s3, w_ref, wo_ref, wa_ref, wl_ref,
-                   v_ref, t_ref, stiff_ref, project_ref, lift_ref, dofs_ref, star_ref, lists_ref, sems):
+def predict_kernel(axes, *refs):
+    sources, (stiff_ref, project_ref, lift_ref, sems), refs = refs[:12], refs[31:35], refs[12:31] + refs[35:]
+    first_ref, late_ref, s0, s1, s2, s3, w_ref, wo_ref, wa_ref, wl_ref = refs[:10]
+    kept, tiles = refs[10:19], refs[19:]
+    dofs_ref, star_ref, lists_ref = kept[:3]
+    v_refs, t_refs = tiles[::2], tiles[1::2]
     h = step_length
     rows = first_ref.shape[1]
-    pairs = [(stiff_in, stiff_ref), (project_in, project_ref), (lift_in, lift_ref),
-             (dofs_in, dofs_ref), (star_in, star_ref), (lists_in, lists_ref)]
-    copies = [pltpu.make_async_copy(src, dst, sems.at[i]) for i, (src, dst) in enumerate(pairs)]
+    targets = (stiff_ref, project_ref, lift_ref) + tuple(kept)
+    copies = [pltpu.make_async_copy(src, dst, sems.at[i]) for i, (src, dst) in enumerate(zip(sources, targets))]
     for copy in copies:
         copy.start()
     for copy in copies[:3]:
@@ -176,10 +187,12 @@
     wl_ref[...] = lift_weights(lift_ref, rows)
     copies[3].wait()
     for q in range(dofs_ref.shape[0]):
-        v_ref[q] = pad_rows(dofs_ref[q], rows)
+        for i, v_ref in enumerate(v_refs):
+            v_ref[q] = pad_rows(dofs_ref[q, :, i * LANES : (i + 1) * LANES], rows)
     sums = [(first_ref, weights_of(0.0, h)), (late_ref, weights_of(h, 2 * h))]
-    series(w_ref, v_ref, t_ref, star_ref, sums, copies[4].wait)
-    copies[5].wait()
+    series(w_ref, v_refs, t_refs, star_ref, sums, copies[4].wait)
+    for copy in copies[5:]:
+        copy.wait()
     pack_sends(first_ref, lists_ref, [s0, s1, s2, s3], parities(axes))
 
 
@@ -262,17 +275,16 @@
     return acc
 
 
-def gather(operand, index, picked_ref):
+def gather(operand, index, picked_ref, other_ref=None):
     faces, n = index.shape
     picks = [(iota((operand.shape[1], n), 0) == index[f : f + 1]).astype(bf16) for f in range(faces)]
-    picked_ref[...] = jnp.dot(operand, jnp.concatenate(picks, axis=1), preferred_element_type=f32)
+    got = jnp.dot(operand, jnp.concatenate(picks, axis=1), preferred_element_type=f32)
+    picked_ref[...] = got if other_ref is None else got + other_ref[...]
     return [picked_ref.at[:, f * n : (f + 1) * n] for f in range(faces)]
 
 
-def own_kernel(own_ref, star_ref, minus_in, w_ref, wa_ref, near_ref, face_ref, type_ref,
-               part_ref, g_ref, across_ref, trace_ref, t_ref, picked_ref, minus_ref, sem):
-    minus_copy = pltpu.make_async_copy(minus_in, minus_ref, sem)
-    minus_copy.start()
+def own_kernel(own_ref, star_ref, minus_ref, w_ref, near_ref, face_ref, type_ref,
+               part_ref, g_ref, picked_ref, trace_ref, t_ref):
     quantities, rows, n = own_ref.shape
     tall = trace_ref.shape[1]
     groups = quantities // 3
@@ -287,16 +299,9 @@
             start = 9 * rows + i * tall
             trace_ref[3 * g + i] = t[start : start + tall, g * n : (g + 1) * n]
 
-    index, source = effective(type_ref, near_ref, face_ref)
+    index, _ = effective(type_ref, near_ref, face_ref)
     high, low = split(stacked(own_ref, 0, quantities))
-    picked = gather(jnp.concatenate([high, low], axis=0), index, picked_ref)
-
-    def keep(q, value):
-        across_ref[q] = value
-
-    across_traces(wa_ref, picked, source, quantities, rows, keep)
-
-    minus_copy.wait()
+    gather(jnp.concatenate([high, low], axis=0), index, picked_ref)
 
     def tile(lane):
         acc = star_mix(star_ref, t_ref, lane, quantities)
@@ -317,7 +322,7 @@
 
 
 def ghost_part(axes, got_refs, plus_ref, wa_ref, wl_ref, near_ref, face_ref, type_ref,
-               part_ref, g_ref, across_ref, picked_ref, trace_ref, flux_ref, emit):
+               part_ref, g_ref, own_picked_ref, picked_ref, trace_ref, flux_ref, emit):
     quantities, rows, n = part_ref.shape
     count = got_refs[0].shape[2]
     index, source = effective(type_ref, near_ref, face_ref)
@@ -333,10 +338,10 @@
         both = jnp.concatenate([high, low], axis=0)
         empty = jnp.zeros((both.shape[0], LANES - count), bf16)
         operands.append(jnp.concatenate([both, empty], axis=1))
-    picked = gather(jnp.concatenate(operands, axis=1), column, picked_ref)
+    picked = gather(jnp.concatenate(operands, axis=1), column, picked_ref, own_picked_ref)
 
     def keep(q, value):
-        trace_ref[q] = across_ref[q] + value
+        trace_ref[q] = value
 
     across_traces(wa_ref, picked, source, quantities, rows, keep)
 
@@ -358,26 +363,22 @@
 
 
 def middle_kernel(axes, got0, got1, got2, got3, plus_ref, wa_ref, wl_ref, near_ref, face_ref, type_ref,
-                  part_ref, g_ref, across_ref, dofs_ref, star_ref, w_ref, cluster_in, late_ref, lists_in,
+                  part_ref, g_ref, own_picked_ref, dofs_ref, star_ref, w_ref, cluster_ref, late_ref, lists_ref,
                   midway_ref, second_ref, s0, s1, s2, s3,
-                  picked_ref, trace_ref, flux_ref, v_ref, t_ref, cluster_ref, lists_ref, sems):
-    copies = [pltpu.make_async_copy(cluster_in, cluster_ref, sems.at[0]),
-              pltpu.make_async_copy(lists_in, lists_ref, sems.at[1])]
-    for copy in copies:
-        copy.start()
+                  picked_ref, trace_ref, flux_ref, *tiles):
+    v_refs, t_refs = tiles[::2], tiles[1::2]
     rows = part_ref.shape[1]
     quantities = part_ref.shape[0]
 
     def emit(q, change):
         value = pad_rows(dofs_ref[q], rows) + change
         midway_ref[q] = value
-        v_ref[q] = value
+        for i, v_ref in enumerate(v_refs):
+            v_ref[q] = value[:, i * LANES : (i + 1) * LANES]
 
     ghost_part(axes, [got0, got1, got2, got3], plus_ref, wa_ref, wl_ref, near_ref, face_ref, type_ref,
-               part_ref, g_ref, across_ref, picked_ref, trace_ref, flux_ref, emit)
-    series(w_ref, v_ref, t_ref, star_ref, [(second_ref, weights_of(0.0, step_length))])
-    for copy in copies:
-        copy.wait()
+               part_ref, g_ref, own_picked_ref, picked_ref, trace_ref, flux_ref, emit)
+    series(w_ref, v_refs, t_refs, star_ref, [(second_ref, weights_of(0.0, step_length))])
     fast = cluster_ref[...][None, :] == 0
     for q in range(quantities):
         second_ref[q] = jnp.where(fast, second_ref[q], late_ref[q])
@@ -385,14 +386,14 @@
 
 
 def finish_kernel(axes, got0, got1, got2, got3, plus_ref, wa_ref, wl_ref, near_ref, face_ref, type_ref,
-                  part_ref, g_ref, across_ref, midway_ref, out_ref, picked_ref, trace_ref, flux_ref):
+                  part_ref, g_ref, own_picked_ref, midway_ref, out_ref, picked_ref, trace_ref, flux_ref):
     count = out_ref.shape[1]
 
     def emit(q, change):
         out_ref[q] = (midway_ref[q] + change)[:count]
 
     ghost_part(axes, [got0, got1, got2, got3], plus_ref, wa_ref, wl_ref, near_ref, face_ref, type_ref,
-               part_ref, g_ref, across_ref, picked_ref, trace_ref, flux_ref, emit)
+               part_ref, g_ref, own_picked_ref, picked_ref, trace_ref, flux_ref, emit)
 
 
 def call(kernel, name, args, outs, scratch, flops, far=(), vmem_bytes=20 << 20):
@@ -451,41 +452,42 @@
         jax.ShapeDtypeStruct((faces * tall, 3 * faces * count), bf16),
         jax.ShapeDtypeStruct((2 * rows, 6 * tall), bf16),
     )
-    v_field = pltpu.VMEM((quantities, rows, n), f32)
+    tiles = [pltpu.VMEM((quantities, rows, LANES), f32), pltpu.VMEM((3 * quantities, rows, LANES), f32)] * (n // LANES)
     t_field = pltpu.VMEM((3 * quantities, rows, n), f32)
     t_trace = pltpu.VMEM((quantities, tall, n), f32)
     picked = pltpu.VMEM((2 * quantities * rows, faces * n), f32)
 
-    inputs = (stiffness, project, lift, dofs, star, send_list)
+    local = (stiffness, project, lift)
+    kept = (dofs, star, send_list, minus, plus, neighbour, neighbour_face, face_type, cluster)
+    inputs = local + kept
     first, late, *out = call(
-        functools.partial(predict_kernel, axes), "predict", inputs, (field, field, *sends, *weights),
-        [v_field, t_field] + [pltpu.VMEM(a.shape, a.dtype) for a in inputs]
-        + [pltpu.SemaphoreType.DMA((len(inputs),))], 10_000_000, far=range(len(inputs)))
-    out, (w, wo, wa, wl) = out[:DIRS], out[DIRS:]
+        functools.partial(predict_kernel, axes), "predict", inputs,
+        (field, field, *sends, *weights, *(jax.ShapeDtypeStruct(a.shape, a.dtype) for a in kept)),
+        [pltpu.VMEM(a.shape, a.dtype) for a in local] + [pltpu.SemaphoreType.DMA((len(inputs),))] + tiles,
+        10_000_000, far=range(len(inputs)))
+    out, (w, wo, wa, wl), kept = out[:DIRS], out[DIRS : 2 * DIRS], out[2 * DIRS :]
+    dofs, star, send_list, minus, plus, neighbour, neighbour_face, face_type, cluster = kept
 
     def own(buffer, name):
         return call(
-            own_kernel, name, (buffer, star, minus, wo, wa, neighbour, neighbour_face, face_type),
-            (field, traces, traces),
-            [t_trace, t_field, picked, pltpu.VMEM(minus.shape, f32), pltpu.SemaphoreType.DMA(())],
-            10_000_000, far=(2,))
+            own_kernel, name, (buffer, star, minus, wo, neighbour, neighbour_face, face_type),
+            (field, traces, jax.ShapeDtypeStruct((2 * quantities * rows, faces * n), f32)),
+            [t_trace, t_field], 10_000_000)
 
     ghost_scratch = [picked, t_trace, t_trace]
     got = swap(out)
-    part, g, across = own(first, "own_first")
+    part, g, chosen = own(first, "own_first")
     midway, second, *out = call(
         functools.partial(middle_kernel, axes), "middle",
-        (*got, plus, wa, wl, neighbour, neighbour_face, face_type, part, g, across, dofs, star, w,
+        (*got, plus, wa, wl, neighbour, neighbour_face, face_type, part, g, chosen, dofs, star, w,
          cluster, late, send_list),
         (field, field, *sends),
-        ghost_scratch + [v_field, t_field, pltpu.VMEM((n,), jnp.int32), pltpu.VMEM(send_list.shape, jnp.int32),
-                         pltpu.SemaphoreType.DMA((2,))],
-        10_000_000, far=(16, 18))
+        ghost_scratch + tiles, 10_000_000)
     got = swap(out)
-    part, g, across = own(second, "own_second")
+    part, g, chosen = own(second, "own_second")
     (result,) = call(
         functools.partial(finish_kernel, axes), "finish",
-        (*got, plus, wa, wl, neighbour, neighbour_face, face_type, part, g, across, midway),
+        (*got, plus, wa, wl, neighbour, neighbour_face, face_type, part, g, chosen, midway),
         (jax.ShapeDtypeStruct((quantities, count, n), f32),), ghost_scratch, 10_000_000)
     return result
 

time: 38 us -> 37.2 us (0.979)
  Pallas kernels: 20.6 us -> 19.4 us
  waiting for transfers between devices: 0.04 us -> 0.59 us
    pallas_call x5, Pallas kernels: 20.6 us -> 19.4 us  [call(): pl.pallas_call(kernel, out_shape=[jax.ShapeDtypeStruct(s.shape, s.dtype)...]
    ppermute x8, waiting for transfers between devices: 0.04 us -> 0.59 us  [exchange(): return lax.ppermute(block, axis, route)]
  transfers between devices with their start and end apart: 8 -> 8, of which waited for: 0 -> 1; matrix products, arithmetic and copies ran while one was open for 0% -> 0% of each run, Pallas kernels for 15% -> 13%
where the time goes in v3:
time: 37.2 us; the launch traced here: 37 us
  Pallas kernels  19.4 us (52%)
  starting transfers between devices  16.8 us (45%)
  waiting for transfers between devices  0.59 us (2%)
    pallas_call x5, Pallas kernels, call(): pl.pallas_call(kernel, out_shape=[jax.ShapeDtypeStruct(s.shape, s.dtype)...  19.4 us
    ppermute x8, starting transfers between devices, exchange(): return lax.ppermute(block, axis, route)  16.8 us
  transfers between devices with their start and end apart: 8, of which 1 were waited for; matrix products, arithmetic and copies ran while one was open for 0% of the time, Pallas kernels for 13%

profile of v3, /device:TPU:13, one launch (start us, length us, event | category | flops | bytes accessed | tf_op | source)
XLA Modules:
  0.0 37.0 jit_solution(1459094375392234643)
XLA Ops:
  0.0 5.8 %predict.1 = (f32[9,24,384]{2,1,0:T(8,128)S(1)}, f32[9,24,384]{2,1,0:T(8,128)S(1)}, f32[9,24,96]{2,1,0:T(8,128)S(1)}, f32[9,24,96]{2,1,0:T(8,128)S(1)}, f32[9,24...) custom-call(f32[3,20,20]{2,1,0:T(8,128)} %refs_0_.1, ...), custom_call_target="tpu_custom_call" | custom-call | flops 10000000 | bytes 5016256 | tf_op jit(solution)/shard_map/predict/pallas_call | solution.py:403
  5.8 0.3 collective-permute-start
  6.1 4.1 %collective-permute-start.1 = (f32[9,24,96]{2,1,0:T(8,128)S(1)}, f32[9,24,96]{2,1,0:T(8,128)S(1)}, u32[]{:S(2)}, u32[]{:S(2)}) collective-permute-start(f32[9,24,96]{2,1,0:T(8,128)S(1)} %get-tuple-element.37), channel_id=1, source_target_pairs={{4,8},{8,4},{12,16},{16,12},{20,24},{24,20},{5,9},{9,5},{13,17},{1... | collective-permute-start | bytes 248840 | tf_op jit(solution)/shard_map/ppermute | solution.py:420
  10.2 1.3 %collective-permute-start.2 = (f32[9,24,96]{2,1,0:T(8,128)S(1)}, f32[9,24,96]{2,1,0:T(8,128)S(1)}, u32[]{:S(2)}, u32[]{:S(2)}) collective-permute-start(f32[9,24,96]{2,1,0:T(8,128)S(1)} %get-tuple-element.38), channel_id=1, source_target_pairs={{0,1},{1,0},{2,3},{3,2},{4,5},{5,4},{6,7},{7,6},{8,9},{9,8},{10,11... | collective-permute-start | bytes 248840 | tf_op jit(solution)/shard_map/ppermute | solution.py:420
  11.5 3.0 %collective-permute-start.3 = (f32[9,24,96]{2,1,0:T(8,128)S(1)}, f32[9,24,96]{2,1,0:T(8,128)S(1)}, u32[]{:S(2)}, u32[]{:S(2)}) collective-permute-start(f32[9,24,96]{2,1,0:T(8,128)S(1)} %get-tuple-element.39), channel_id=1, source_target_pairs={{1,2},{2,1},{5,6},{6,5},{9,10},{10,9},{13,14},{14,13},{17,18},{18,... | collective-permute-start | bytes 248840 | tf_op jit(solution)/shard_map/ppermute | solution.py:420
  14.6 2.4 %own_first.1 = (f32[9,24,384]{2,1,0:T(8,128)S(1)}, f32[9,40,384]{2,1,0:T(8,128)S(1)}, f32[432,1536]{1,0:T(8,128)S(1)}) custom-call(f32[9,24,384]{2,1,0:T(8,128)S(1)} %get-tuple-element.46.own_ref, f32[9,9,3,384]{3,2,1,0:T(4,128)S(1)} %get-tuple-element.47.star_ref, f32[9,9,4,384]{3,2,1,0:T(4,128)S(1)} %get-tuple-element.48.minus_ref, ...), custom_call_target="tpu_custom_call" | custom-call | flops 10000000 | bytes 5050368 | tf_op jit(solution)/shard_map/own_first/pallas_call | solution.py:403
  17.0 0.0 collective-permute-done.got0
  17.0 0.0 collective-permute-done.1.got1
  17.0 0.0 collective-permute-done.2.got2
  17.0 0.6 %collective-permute-done.3.got3 = f32[9,24,96]{2,1,0:T(8,128)S(1)} collective-permute-done((f32[9,24,96]{2,1,0:T(8,128)S(1)}, f32[9,24,96]{2,1,0:T(8,128)S(1)}, u32[]{:S(2)}, u32[]{:S(2)}) %collective-permute-start.3) | collective-permute-done | bytes 82976 | tf_op jit(solution)/shard_map/ppermute | solution.py:420
  17.6 6.0 %middle.1 = (f32[9,24,384]{2,1,0:T(8,128)S(1)}, f32[9,24,384]{2,1,0:T(8,128)S(1)}, f32[9,24,96]{2,1,0:T(8,128)S(1)}, f32[9,24,96]{2,1,0:T(8,128)S(1)}, f32[9,24,...) custom-call(f32[9,24,96]{2,1,0:T(8,128)S(1)} %collective-permute-done.got0, f32[9,24,96]{2,1,0:T(8,128)S(1)} %collective-permute-done.1.got1, ...), custom_call_target="tpu_custom_call" | custom-call | flops 10000000 | bytes 6753024 | tf_op jit(solution)/shard_map/middle/pallas_call | solution.py:403
  23.6 0.1 collective-permute-start.4
  23.6 4.4 %collective-permute-start.5 = (f32[9,24,96]{2,1,0:T(8,128)S(1)}, f32[9,24,96]{2,1,0:T(8,128)S(1)}, u32[]{:S(2)}, u32[]{:S(2)}) collective-permute-start(f32[9,24,96]{2,1,0:T(8,128)S(1)} %get-tuple-element.59), channel_id=1, source_target_pairs={{4,8},{8,4},{12,16},{16,12},{20,24},{24,20},{5,9},{9,5},{13,17},{1... | collective-permute-start | bytes 248840 | tf_op jit(solution)/shard_map/ppermute | solution.py:420
  28.0 0.1 collective-permute-start.6
  28.1 3.6 %collective-permute-start.7 = (f32[9,24,96]{2,1,0:T(8,128)S(1)}, f32[9,24,96]{2,1,0:T(8,128)S(1)}, u32[]{:S(2)}, u32[]{:S(2)}) collective-permute-start(f32[9,24,96]{2,1,0:T(8,128)S(1)} %get-tuple-element.61), channel_id=1, source_target_pairs={{1,2},{2,1},{5,6},{6,5},{9,10},{10,9},{13,14},{14,13},{17,18},{18,... | collective-permute-start | bytes 248840 | tf_op jit(solution)/shard_map/ppermute | solution.py:420
  31.7 2.4 %own_second.1 = (f32[9,24,384]{2,1,0:T(8,128)S(1)}, f32[9,40,384]{2,1,0:T(8,128)S(1)}, f32[432,1536]{1,0:T(8,128)S(1)}) custom-call(f32[9,24,384]{2,1,0:T(8,128)S(1)} %get-tuple-element.62.own_ref, f32[9,9,3,384]{3,2,1,0:T(4,128)S(1)} %get-tuple-element.47.star_ref, f32[9,9,4,384]{3,2,1,0:T(4,128)S(1)} %get-tuple-element.48.minus_ref, ...), custom_call_target="tpu_custom_call" | custom-call | flops 10000000 | bytes 5050368 | tf_op jit(solution)/shard_map/own_second/pallas_call | solution.py:403
  34.1 0.0 collective-permute-done.4.got0
  34.1 0.0 collective-permute-done.5.got1
  34.1 0.0 collective-permute-done.6.got2
  34.1 0.0 collective-permute-done.7.got3
  34.2 2.8 %finish.1 = f32[9,20,384]{2,1,0:T(8,128)} custom-call(f32[9,24,96]{2,1,0:T(8,128)S(1)} %collective-permute-done.4.got0, f32[9,24,96]{2,1,0:T(8,128)S(1)} %collective-permute-done.5.got1, f32[9,24,96]{2,1,0:T(8,128)S(1)} %collective-permute-done.6.got2, f32[9,24,96]{2,1,0:T(8,128)S(1)} %collective-permute-done.7.got3, ...), custom_call_target="tpu_custom_call" | custom-call | flops 10000000 | bytes 5194752 | tf_op jit(solution)/shard_map/finish/pallas_call | solution.py:403
Async XLA Ops:
  5.8 11.2 %collective-permute-start = (f32[9,24,96]{2,1,0:T(8,128)S(1)}, f32[9,24,96]{2,1,0:T(8,128)S(1)}, u32[]{:S(2)}, u32[]{:S(2)}) collective-permute-start(f32[9,24,96]{2,1,0:T(8,128)S(1)} %get-tuple-element.36), channel_id=1, source_target_pairs={{0,4},{4,0},{8,12},{12,8},{16,20},{20,16},{24,28},{28,24},{1,5},{5... | collective-permute-start | bytes 248840 | tf_op jit(solution)/shard_map/ppermute | solution.py:420
  6.1 10.9 %collective-permute-start.1 = (f32[9,24,96]{2,1,0:T(8,128)S(1)}, f32[9,24,96]{2,1,0:T(8,128)S(1)}, u32[]{:S(2)}, u32[]{:S(2)}) collective-permute-start(f32[9,24,96]{2,1,0:T(8,128)S(1)} %get-tuple-element.37), channel_id=1, source_target_pairs={{4,8},{8,4},{12,16},{16,12},{20,24},{24,20},{5,9},{9,5},{13,17},{1... | collective-permute-start | bytes 248840 | tf_op jit(solution)/shard_map/ppermute | solution.py:420
  10.2 6.8 %collective-permute-start.2 = (f32[9,24,96]{2,1,0:T(8,128)S(1)}, f32[9,24,96]{2,1,0:T(8,128)S(1)}, u32[]{:S(2)}, u32[]{:S(2)}) collective-permute-start(f32[9,24,96]{2,1,0:T(8,128)S(1)} %get-tuple-element.38), channel_id=1, source_target_pairs={{0,1},{1,0},{2,3},{3,2},{4,5},{5,4},{6,7},{7,6},{8,9},{9,8},{10,11... | collective-permute-start | bytes 248840 | tf_op jit(solution)/shard_map/ppermute | solution.py:420
  11.5 6.1 %collective-permute-start.3 = (f32[9,24,96]{2,1,0:T(8,128)S(1)}, f32[9,24,96]{2,1,0:T(8,128)S(1)}, u32[]{:S(2)}, u32[]{:S(2)}) collective-permute-start(f32[9,24,96]{2,1,0:T(8,128)S(1)} %get-tuple-element.39), channel_id=1, source_target_pairs={{1,2},{2,1},{5,6},{6,5},{9,10},{10,9},{13,14},{14,13},{17,18},{18,... | collective-permute-start | bytes 248840 | tf_op jit(solution)/shard_map/ppermute | solution.py:420
  23.6 10.6 %collective-permute-start.4 = (f32[9,24,96]{2,1,0:T(8,128)S(1)}, f32[9,24,96]{2,1,0:T(8,128)S(1)}, u32[]{:S(2)}, u32[]{:S(2)}) collective-permute-start(f32[9,24,96]{2,1,0:T(8,128)S(1)} %get-tuple-element.58), channel_id=1, source_target_pairs={{0,4},{4,0},{8,12},{12,8},{16,20},{20,16},{24,28},{28,24},{1,5},{5... | collective-permute-start | bytes 248840 | tf_op jit(solution)/shard_map/ppermute | solution.py:420
  23.6 10.5 %collective-permute-start.5 = (f32[9,24,96]{2,1,0:T(8,128)S(1)}, f32[9,24,96]{2,1,0:T(8,128)S(1)}, u32[]{:S(2)}, u32[]{:S(2)}) collective-permute-start(f32[9,24,96]{2,1,0:T(8,128)S(1)} %get-tuple-element.59), channel_id=1, source_target_pairs={{4,8},{8,4},{12,16},{16,12},{20,24},{24,20},{5,9},{9,5},{13,17},{1... | collective-permute-start | bytes 248840 | tf_op jit(solution)/shard_map/ppermute | solution.py:420
  28.0 6.1 %collective-permute-start.6 = (f32[9,24,96]{2,1,0:T(8,128)S(1)}, f32[9,24,96]{2,1,0:T(8,128)S(1)}, u32[]{:S(2)}, u32[]{:S(2)}) collective-permute-start(f32[9,24,96]{2,1,0:T(8,128)S(1)} %get-tuple-element.60), channel_id=1, source_target_pairs={{0,1},{1,0},{2,3},{3,2},{4,5},{5,4},{6,7},{7,6},{8,9},{9,8},{10,11... | collective-permute-start | bytes 248840 | tf_op jit(solution)/shard_map/ppermute | solution.py:420
  28.1 6.1 %collective-permute-start.7 = (f32[9,24,96]{2,1,0:T(8,128)S(1)}, f32[9,24,96]{2,1,0:T(8,128)S(1)}, u32[]{:S(2)}, u32[]{:S(2)}) collective-permute-start(f32[9,24,96]{2,1,0:T(8,128)S(1)} %get-tuple-element.61), channel_id=1, source_target_pairs={{1,2},{2,1},{5,6},{6,5},{9,10},{10,9},{13,14},{14,13},{17,18},{18,... | collective-permute-start | bytes 248840 | tf_op jit(solution)/shard_map/ppermute | solution.py:420

commit v4 on v3

--- a/solution.py
+++ b/solution.py
@@ -58,29 +58,61 @@
     return [jnp.where(owner == q, both, 0.0) for q in range(copies)]
 
 
+MAIN = 16
+
+
+def rest_pairs():
+    return [(k, k + 1 if k + 1 < 9 else None) for k in range(0, 9, 2)]
+
+
 def series_weights(stiff_ref, rows, transposed):
-    out = []
+    blocks = []
     for c in range(3):
-        for block in block_weights(stiff_ref[c], rows, 3, transposed):
-            out.append(pad_rows(block, rows))
+        blocks += block_weights(stiff_ref[c], rows, 3, transposed)
+    out = [block[:MAIN] for block in blocks]
+    for one, other in rest_pairs():
+        tail = blocks[one][MAIN:]
+        out += [tail, jnp.zeros_like(tail) if other is None else blocks[other][MAIN:]]
     return jnp.concatenate(out, axis=0).astype(bf16)
+
+
+def rest_factors(star_ref, out_ref):
+    quantities, _, _, n = star_ref.shape
+    lower = iota((8, n), 0) < 4
+    for p in range(quantities):
+        for g in range(quantities // 3):
+            for k, (one, other) in enumerate(rest_pairs()):
+                c, q = one // 3, 3 * g + one % 3
+                value = jnp.broadcast_to(star_ref[p, q, c : c + 1], (8, n))
+                if other is not None:
+                    c, q = other // 3, 3 * g + other % 3
+                    value = jnp.where(lower, value, jnp.broadcast_to(star_ref[p, q, c : c + 1], (8, n)))
+                out_ref[p, g * 5 + k] = value
 
 
 def stacked(ref, first, count):
     return jnp.concatenate([ref[first + i] for i in range(count)], axis=0)
 
 
-def star_mix(star_ref, t_ref, lane, quantities):
-    rows = t_ref.shape[1]
+def star_mix(star_ref, rest_ref, t_ref, lane, quantities):
     within = lane if t_ref.shape[2] > LANES else pl.ds(0, LANES)
-    acc = [None] * quantities
-    for c in range(3):
-        for q in range(quantities):
-            t = t_ref[c * quantities + q, :, within]
+    acc, tails = [None] * quantities, [None] * quantities
+    for g in range(quantities // 3):
+        for k in range(9):
+            t = t_ref[g, k * MAIN : (k + 1) * MAIN, within]
+            c, q = k // 3, 3 * g + k % 3
             for p in range(quantities):
-                term = jnp.broadcast_to(star_ref[p, q, c : c + 1, lane], (rows, LANES)) * t
+                term = jnp.broadcast_to(star_ref[p, q, c : c + 1, lane], (MAIN, LANES)) * t
                 acc[p] = term if acc[p] is None else acc[p] + term
-    return acc
+        for k in range(5):
+            start = 9 * MAIN + 8 * k
+            t = t_ref[g, start : start + 8, within]
+            for p in range(quantities):
+                term = rest_ref[p, g * 5 + k, :, lane] * t
+                tails[p] = term if tails[p] is None else tails[p] + term
+    return [
+        jnp.concatenate([a, tail + pltpu.roll(tail, 4, 0)], axis=0) for a, tail in zip(acc, tails)
+    ]
 
 
 def lane_tiles(n, body):
@@ -92,16 +124,11 @@
 
 
 def stiff_products(w_ref, v_ref, t_ref):
-    quantities, rows = v_ref.shape[:2]
-    for g in range(quantities // 3):
-        t = jnp.dot(w_ref[...], triple(stacked(v_ref, 3 * g, 3)), preferred_element_type=f32)
-        for c in range(3):
-            for i in range(3):
-                start = (3 * c + i) * rows
-                t_ref[c * quantities + 3 * g + i] = t[start : start + rows]
-
-
-def series(w_ref, v_refs, t_refs, star_ref, sums, ready=lambda: None):
+    for g in range(v_ref.shape[0] // 3):
+        t_ref[g] = jnp.dot(w_ref[...], triple(stacked(v_ref, 3 * g, 3)), preferred_element_type=f32)
+
+
+def series(w_ref, v_refs, t_refs, star_ref, rest_ref, sums, ready=lambda: None):
     quantities = v_refs[0].shape[0]
     lanes = [pl.ds(i * LANES, LANES) for i in range(len(v_refs))]
     for v_ref, t_ref, lane in zip(v_refs, t_refs, lanes):
@@ -118,7 +145,7 @@
             return jnp.where(degree == 0, weights[1], weights[2])
 
         for v_ref, t_ref, lane in zip(v_refs, t_refs, lanes):
-            acc = star_mix(star_ref, t_ref, lane, quantities)
+            acc = star_mix(star_ref, rest_ref, t_ref, lane, quantities)
             for p in range(quantities):
                 value = -acc[p]
                 if not last:
@@ -165,9 +192,9 @@
 
 
 def predict_kernel(axes, *refs):
-    sources, (stiff_ref, project_ref, lift_ref, sems), refs = refs[:12], refs[31:35], refs[12:31] + refs[35:]
+    sources, (stiff_ref, project_ref, lift_ref, sems), refs = refs[:12], refs[32:36], refs[12:32] + refs[36:]
     first_ref, late_ref, s0, s1, s2, s3, w_ref, wo_ref, wa_ref, wl_ref = refs[:10]
-    kept, tiles = refs[10:19], refs[19:]
+    kept, rest_ref, tiles = refs[10:19], refs[19], refs[20:]
     dofs_ref, star_ref, lists_ref = kept[:3]
     v_refs, t_refs = tiles[::2], tiles[1::2]
     h = step_length
@@ -181,8 +208,9 @@
     faces_basis = project_ref.shape[0]
     flat = jnp.concatenate([project_ref[b] for b in range(faces_basis)], axis=0)
     w_ref[...] = series_weights(stiff_ref, rows, False)
-    wo_ref[: 9 * rows] = series_weights(stiff_ref, rows, True)
-    wo_ref[9 * rows :] = jnp.concatenate(block_weights(flat, rows, 3, False), axis=0).astype(bf16)
+    height = w_ref.shape[0]
+    wo_ref[:height] = series_weights(stiff_ref, rows, True)
+    wo_ref[height:] = jnp.concatenate(block_weights(flat, rows, 3, False), axis=0).astype(bf16)
     wa_ref[...] = across_weights(project_ref)
     wl_ref[...] = lift_weights(lift_ref, rows)
     copies[3].wait()
@@ -190,7 +218,11 @@
         for i, v_ref in enumerate(v_refs):
             v_ref[q] = pad_rows(dofs_ref[q, :, i * LANES : (i + 1) * LANES], rows)
     sums = [(first_ref, weights_of(0.0, h)), (late_ref, weights_of(h, 2 * h))]
-    series(w_ref, v_refs, t_refs, star_ref, sums, copies[4].wait)
+    def ready():
+        copies[4].wait()
+        rest_factors(star_ref, rest_ref)
+
+    series(w_ref, v_refs, t_refs, star_ref, rest_ref, sums, ready)
     for copy in copies[5:]:
         copy.wait()
     pack_sends(first_ref, lists_ref, [s0, s1, s2, s3], parities(axes))
@@ -283,20 +315,18 @@
     return [picked_ref.at[:, f * n : (f + 1) * n] for f in range(faces)]
 
 
-def own_kernel(own_ref, star_ref, minus_ref, w_ref, near_ref, face_ref, type_ref,
+def own_kernel(own_ref, star_ref, rest_ref, minus_ref, w_ref, near_ref, face_ref, type_ref,
                part_ref, g_ref, picked_ref, trace_ref, t_ref):
     quantities, rows, n = own_ref.shape
     tall = trace_ref.shape[1]
     groups = quantities // 3
     x = jnp.concatenate([triple(stacked(own_ref, 3 * g, 3)) for g in range(groups)], axis=1)
     t = jnp.dot(w_ref[...], x, preferred_element_type=f32)
+    height = t_ref.shape[1]
     for g in range(groups):
-        for c in range(3):
-            for i in range(3):
-                start = (3 * c + i) * rows
-                t_ref[c * quantities + 3 * g + i] = t[start : start + rows, g * n : (g + 1) * n]
+        t_ref[g] = t[:height, g * n : (g + 1) * n]
         for i in range(3):
-            start = 9 * rows + i * tall
+            start = height + i * tall
             trace_ref[3 * g + i] = t[start : start + tall, g * n : (g + 1) * n]
 
     index, _ = effective(type_ref, near_ref, face_ref)
@@ -304,7 +334,7 @@
     gather(jnp.concatenate([high, low], axis=0), index, picked_ref)
 
     def tile(lane):
-        acc = star_mix(star_ref, t_ref, lane, quantities)
+        acc = star_mix(star_ref, rest_ref, t_ref, lane, quantities)
         for p in range(quantities):
             part_ref[p, :, lane] = acc[p]
         acc = flux_mix(minus_ref, trace_ref, lane, [None] * quantities)
@@ -363,7 +393,7 @@
 
 
 def middle_kernel(axes, got0, got1, got2, got3, plus_ref, wa_ref, wl_ref, near_ref, face_ref, type_ref,
-                  part_ref, g_ref, own_picked_ref, dofs_ref, star_ref, w_ref, cluster_ref, late_ref, lists_ref,
+                  part_ref, g_ref, own_picked_ref, dofs_ref, star_ref, rest_ref, w_ref, cluster_ref, late_ref, lists_ref,
                   midway_ref, second_ref, s0, s1, s2, s3,
                   picked_ref, trace_ref, flux_ref, *tiles):
     v_refs, t_refs = tiles[::2], tiles[1::2]
@@ -378,7 +408,7 @@
 
     ghost_part(axes, [got0, got1, got2, got3], plus_ref, wa_ref, wl_ref, near_ref, face_ref, type_ref,
                part_ref, g_ref, own_picked_ref, picked_ref, trace_ref, flux_ref, emit)
-    series(w_ref, v_refs, t_refs, star_ref, [(second_ref, weights_of(0.0, step_length))])
+    series(w_ref, v_refs, t_refs, star_ref, rest_ref, [(second_ref, weights_of(0.0, step_length))])
     fast = cluster_ref[...][None, :] == 0
     for q in range(quantities):
         second_ref[q] = jnp.where(fast, second_ref[q], late_ref[q])
@@ -446,14 +476,16 @@
     field = jax.ShapeDtypeStruct((quantities, rows, n), f32)
     traces = jax.ShapeDtypeStruct((quantities, tall, n), f32)
     sends = (jax.ShapeDtypeStruct((quantities, rows, width), f32),) * DIRS
+    height = 9 * MAIN + 8 * len(rest_pairs())
+    groups = quantities // 3
     weights = (
-        jax.ShapeDtypeStruct((9 * rows, 9 * rows), bf16),
-        jax.ShapeDtypeStruct((9 * rows + 3 * tall, 9 * rows), bf16),
+        jax.ShapeDtypeStruct((height, 9 * rows), bf16),
+        jax.ShapeDtypeStruct((height + 3 * tall, 9 * rows), bf16),
         jax.ShapeDtypeStruct((faces * tall, 3 * faces * count), bf16),
         jax.ShapeDtypeStruct((2 * rows, 6 * tall), bf16),
     )
-    tiles = [pltpu.VMEM((quantities, rows, LANES), f32), pltpu.VMEM((3 * quantities, rows, LANES), f32)] * (n // LANES)
-    t_field = pltpu.VMEM((3 * quantities, rows, n), f32)
+    tiles = [pltpu.VMEM((quantities, rows, LANES), f32), pltpu.VMEM((groups, height, LANES), f32)] * (n // LANES)
+    t_field = pltpu.VMEM((groups, height, n), f32)
     t_trace = pltpu.VMEM((quantities, tall, n), f32)
     picked = pltpu.VMEM((2 * quantities * rows, faces * n), f32)
 
@@ -462,15 +494,16 @@
     inputs = local + kept
     first, late, *out = call(
         functools.partial(predict_kernel, axes), "predict", inputs,
-        (field, field, *sends, *weights, *(jax.ShapeDtypeStruct(a.shape, a.dtype) for a in kept)),
+        (field, field, *sends, *weights, *(jax.ShapeDtypeStruct(a.shape, a.dtype) for a in kept),
+         jax.ShapeDtypeStruct((quantities, groups * len(rest_pairs()), 8, n), f32)),
         [pltpu.VMEM(a.shape, a.dtype) for a in local] + [pltpu.SemaphoreType.DMA((len(inputs),))] + tiles,
         10_000_000, far=range(len(inputs)))
     out, (w, wo, wa, wl), kept = out[:DIRS], out[DIRS : 2 * DIRS], out[2 * DIRS :]
-    dofs, star, send_list, minus, plus, neighbour, neighbour_face, face_type, cluster = kept
+    dofs, star, send_list, minus, plus, neighbour, neighbour_face, face_type, cluster, rest = kept
 
     def own(buffer, name):
         return call(
-            own_kernel, name, (buffer, star, minus, wo, neighbour, neighbour_face, face_type),
+            own_kernel, name, (buffer, star, rest, minus, wo, neighbour, neighbour_face, face_type),
             (field, traces, jax.ShapeDtypeStruct((2 * quantities * rows, faces * n), f32)),
             [t_trace, t_field], 10_000_000)
 
@@ -479,7 +512,7 @@
     part, g, chosen = own(first, "own_first")
     midway, second, *out = call(
         functools.partial(middle_kernel, axes), "middle",
-        (*got, plus, wa, wl, neighbour, neighbour_face, face_type, part, g, chosen, dofs, star, w,
+        (*got, plus, wa, wl, neighbour, neighbour_face, face_type, part, g, chosen, dofs, star, rest, w,
          cluster, late, send_list),
         (field, field, *sends),
         ghost_scratch + tiles, 10_000_000)

time: 37.2 us -> 36.8 us (0.989)
  Pallas kernels: 19.4 us -> 18.7 us
    pallas_call x5, Pallas kernels: 19.4 us -> 18.7 us  [call(): pl.pallas_call(kernel, out_shape=[jax.ShapeDtypeStruct(s.shape, s.dtype)...]
  transfers between devices with their start and end apart: 8 -> 8, of which waited for: 1 -> 2; matrix products, arithmetic and copies ran while one was open for 0% -> 0% of each run, Pallas kernels for 13% -> 13%
where the time goes in v4:
time: 36.8 us; the launch traced here: 36.6 us
  Pallas kernels  18.7 us (51%)
  starting transfers between devices  16.8 us (46%)
  waiting for transfers between devices  0.86 us (2%)
    pallas_call x5, Pallas kernels, call(): pl.pallas_call(kernel, out_shape=[jax.ShapeDtypeStruct(s.shape, s.dtype)...  18.7 us
    ppermute x8, starting transfers between devices, exchange(): return lax.ppermute(block, axis, route)  16.8 us
    ppermute x8, waiting for transfers between devices, exchange(): return lax.ppermute(block, axis, route)  0.86 us
  transfers between devices with their start and end apart: 8, of which 2 were waited for; matrix products, arithmetic and copies ran while one was open for 0% of the time, Pallas kernels for 13%

profile of v4, /device:TPU:13, one launch (start us, length us, event | category | flops | bytes accessed | tf_op | source)
XLA Modules:
  0.0 36.6 jit_solution(5916342136538216116)
XLA Ops:
  0.0 5.7 %predict.1 = (f32[9,24,384]{2,1,0:T(8,128)S(1)}, f32[9,24,384]{2,1,0:T(8,128)S(1)}, f32[9,24,96]{2,1,0:T(8,128)S(1)}, f32[9,24,96]{2,1,0:T(8,128)S(1)}, f32[9,24...) custom-call(f32[3,20,20]{2,1,0:T(8,128)} %refs_0_.1, ...), custom_call_target="tpu_custom_call" | custom-call | flops 10000000 | bytes 6619840 | tf_op jit(solution)/shard_map/predict/pallas_call | solution.py:433
  5.7 0.3 collective-permute-start
  6.0 4.1 %collective-permute-start.1 = (f32[9,24,96]{2,1,0:T(8,128)S(1)}, f32[9,24,96]{2,1,0:T(8,128)S(1)}, u32[]{:S(2)}, u32[]{:S(2)}) collective-permute-start(f32[9,24,96]{2,1,0:T(8,128)S(1)} %get-tuple-element.38), channel_id=1, source_target_pairs={{4,8},{8,4},{12,16},{16,12},{20,24},{24,20},{5,9},{9,5},{13,17},{1... | collective-permute-start | bytes 248840 | tf_op jit(solution)/shard_map/ppermute | solution.py:450
  10.2 1.3 %collective-permute-start.2 = (f32[9,24,96]{2,1,0:T(8,128)S(1)}, f32[9,24,96]{2,1,0:T(8,128)S(1)}, u32[]{:S(2)}, u32[]{:S(2)}) collective-permute-start(f32[9,24,96]{2,1,0:T(8,128)S(1)} %get-tuple-element.39), channel_id=1, source_target_pairs={{0,1},{1,0},{2,3},{3,2},{4,5},{5,4},{6,7},{7,6},{8,9},{9,8},{10,11... | collective-permute-start | bytes 248840 | tf_op jit(solution)/shard_map/ppermute | solution.py:450
  11.5 3.0 %collective-permute-start.3 = (f32[9,24,96]{2,1,0:T(8,128)S(1)}, f32[9,24,96]{2,1,0:T(8,128)S(1)}, u32[]{:S(2)}, u32[]{:S(2)}) collective-permute-start(f32[9,24,96]{2,1,0:T(8,128)S(1)} %get-tuple-element.40), channel_id=1, source_target_pairs={{1,2},{2,1},{5,6},{6,5},{9,10},{10,9},{13,14},{14,13},{17,18},{18,... | collective-permute-start | bytes 248840 | tf_op jit(solution)/shard_map/ppermute | solution.py:450
  14.5 2.3 %own_first.1 = (f32[9,24,384]{2,1,0:T(8,128)S(1)}, f32[9,40,384]{2,1,0:T(8,128)S(1)}, f32[432,1536]{1,0:T(8,128)S(1)}) custom-call(f32[9,24,384]{2,1,0:T(8,128)S(1)} %get-tuple-element.47.own_ref, f32[9,9,3,384]{3,2,1,0:T(4,128)S(1)} %get-tuple-element.48.star_ref, f32[9,15,8,384]{3,2,1,0:T(8,128)S(1)} %get-tuple-element.49.rest_ref, ...), custom_call_target="tpu_custom_call" | custom-call | flops 10000000 | bytes 6681600 | tf_op jit(solution)/shard_map/own_first/pallas_call | solution.py:433
  16.8 0.0 collective-permute-done.got0
  16.8 0.0 collective-permute-done.1.got1
  16.8 0.0 collective-permute-done.2.got2
  16.8 0.7 %collective-permute-done.3.got3 = f32[9,24,96]{2,1,0:T(8,128)S(1)} collective-permute-done((f32[9,24,96]{2,1,0:T(8,128)S(1)}, f32[9,24,96]{2,1,0:T(8,128)S(1)}, u32[]{:S(2)}, u32[]{:S(2)}) %collective-permute-start.3) | collective-permute-done | bytes 82976 | tf_op jit(solution)/shard_map/ppermute | solution.py:450
  17.5 5.6 %middle.1 = (f32[9,24,384]{2,1,0:T(8,128)S(1)}, f32[9,24,384]{2,1,0:T(8,128)S(1)}, f32[9,24,96]{2,1,0:T(8,128)S(1)}, f32[9,24,96]{2,1,0:T(8,128)S(1)}, f32[9,24,...) custom-call(f32[9,24,96]{2,1,0:T(8,128)S(1)} %collective-permute-done.got0, f32[9,24,96]{2,1,0:T(8,128)S(1)} %collective-permute-done.1.got1, ...), custom_call_target="tpu_custom_call" | custom-call | flops 10000000 | bytes 8384256 | tf_op jit(solution)/shard_map/middle/pallas_call | solution.py:433
  23.2 0.1 collective-permute-start.4
  23.2 4.4 %collective-permute-start.5 = (f32[9,24,96]{2,1,0:T(8,128)S(1)}, f32[9,24,96]{2,1,0:T(8,128)S(1)}, u32[]{:S(2)}, u32[]{:S(2)}) collective-permute-start(f32[9,24,96]{2,1,0:T(8,128)S(1)} %get-tuple-element.61), channel_id=1, source_target_pairs={{4,8},{8,4},{12,16},{16,12},{20,24},{24,20},{5,9},{9,5},{13,17},{1... | collective-permute-start | bytes 248840 | tf_op jit(solution)/shard_map/ppermute | solution.py:450
  27.6 0.1 collective-permute-start.6
  27.7 3.6 %collective-permute-start.7 = (f32[9,24,96]{2,1,0:T(8,128)S(1)}, f32[9,24,96]{2,1,0:T(8,128)S(1)}, u32[]{:S(2)}, u32[]{:S(2)}) collective-permute-start(f32[9,24,96]{2,1,0:T(8,128)S(1)} %get-tuple-element.63), channel_id=1, source_target_pairs={{1,2},{2,1},{5,6},{6,5},{9,10},{10,9},{13,14},{14,13},{17,18},{18,... | collective-permute-start | bytes 248840 | tf_op jit(solution)/shard_map/ppermute | solution.py:450
  31.3 2.3 %own_second.1 = (f32[9,24,384]{2,1,0:T(8,128)S(1)}, f32[9,40,384]{2,1,0:T(8,128)S(1)}, f32[432,1536]{1,0:T(8,128)S(1)}) custom-call(f32[9,24,384]{2,1,0:T(8,128)S(1)} %get-tuple-element.64.own_ref, f32[9,9,3,384]{3,2,1,0:T(4,128)S(1)} %get-tuple-element.48.star_ref, f32[9,15,8,384]{3,2,1,0:T(8,128)S(1)} %get-tuple-element.49.rest_ref, ...), custom_call_target="tpu_custom_call" | custom-call | flops 10000000 | bytes 6681600 | tf_op jit(solution)/shard_map/own_second/pallas_call | solution.py:433
  33.6 0.0 collective-permute-done.4.got0
  33.6 0.0 collective-permute-done.5.got1
  33.6 0.0 collective-permute-done.6.got2
  33.6 0.1 collective-permute-done.7.got3
  33.8 2.8 %finish.1 = f32[9,20,384]{2,1,0:T(8,128)} custom-call(f32[9,24,96]{2,1,0:T(8,128)S(1)} %collective-permute-done.4.got0, f32[9,24,96]{2,1,0:T(8,128)S(1)} %collective-permute-done.5.got1, f32[9,24,96]{2,1,0:T(8,128)S(1)} %collective-permute-done.6.got2, f32[9,24,96]{2,1,0:T(8,128)S(1)} %collective-permute-done.7.got3, ...), custom_call_target="tpu_custom_call" | custom-call | flops 10000000 | bytes 5194752 | tf_op jit(solution)/shard_map/finish/pallas_call | solution.py:433
Async XLA Ops:
  5.7 11.1 %collective-permute-start = (f32[9,24,96]{2,1,0:T(8,128)S(1)}, f32[9,24,96]{2,1,0:T(8,128)S(1)}, u32[]{:S(2)}, u32[]{:S(2)}) collective-permute-start(f32[9,24,96]{2,1,0:T(8,128)S(1)} %get-tuple-element.37), channel_id=1, source_target_pairs={{0,4},{4,0},{8,12},{12,8},{16,20},{20,16},{24,28},{28,24},{1,5},{5... | collective-permute-start | bytes 248840 | tf_op jit(solution)/shard_map/ppermute | solution.py:450
  6.0 10.8 %collective-permute-start.1 = (f32[9,24,96]{2,1,0:T(8,128)S(1)}, f32[9,24,96]{2,1,0:T(8,128)S(1)}, u32[]{:S(2)}, u32[]{:S(2)}) collective-permute-start(f32[9,24,96]{2,1,0:T(8,128)S(1)} %get-tuple-element.38), channel_id=1, source_target_pairs={{4,8},{8,4},{12,16},{16,12},{20,24},{24,20},{5,9},{9,5},{13,17},{1... | collective-permute-start | bytes 248840 | tf_op jit(solution)/shard_map/ppermute | solution.py:450
  10.2 6.7 %collective-permute-start.2 = (f32[9,24,96]{2,1,0:T(8,128)S(1)}, f32[9,24,96]{2,1,0:T(8,128)S(1)}, u32[]{:S(2)}, u32[]{:S(2)}) collective-permute-start(f32[9,24,96]{2,1,0:T(8,128)S(1)} %get-tuple-element.39), channel_id=1, source_target_pairs={{0,1},{1,0},{2,3},{3,2},{4,5},{5,4},{6,7},{7,6},{8,9},{9,8},{10,11... | collective-permute-start | bytes 248840 | tf_op jit(solution)/shard_map/ppermute | solution.py:450
  11.5 6.1 %collective-permute-start.3 = (f32[9,24,96]{2,1,0:T(8,128)S(1)}, f32[9,24,96]{2,1,0:T(8,128)S(1)}, u32[]{:S(2)}, u32[]{:S(2)}) collective-permute-start(f32[9,24,96]{2,1,0:T(8,128)S(1)} %get-tuple-element.40), channel_id=1, source_target_pairs={{1,2},{2,1},{5,6},{6,5},{9,10},{10,9},{13,14},{14,13},{17,18},{18,... | collective-permute-start | bytes 248840 | tf_op jit(solution)/shard_map/ppermute | solution.py:450
  23.2 10.4 %collective-permute-start.4 = (f32[9,24,96]{2,1,0:T(8,128)S(1)}, f32[9,24,96]{2,1,0:T(8,128)S(1)}, u32[]{:S(2)}, u32[]{:S(2)}) collective-permute-start(f32[9,24,96]{2,1,0:T(8,128)S(1)} %get-tuple-element.60), channel_id=1, source_target_pairs={{0,4},{4,0},{8,12},{12,8},{16,20},{20,16},{24,28},{28,24},{1,5},{5... | collective-permute-start | bytes 248840 | tf_op jit(solution)/shard_map/ppermute | solution.py:450
  23.2 10.4 %collective-permute-start.5 = (f32[9,24,96]{2,1,0:T(8,128)S(1)}, f32[9,24,96]{2,1,0:T(8,128)S(1)}, u32[]{:S(2)}, u32[]{:S(2)}) collective-permute-start(f32[9,24,96]{2,1,0:T(8,128)S(1)} %get-tuple-element.61), channel_id=1, source_target_pairs={{4,8},{8,4},{12,16},{16,12},{20,24},{24,20},{5,9},{9,5},{13,17},{1... | collective-permute-start | bytes 248840 | tf_op jit(solution)/shard_map/ppermute | solution.py:450
  27.6 6.0 %collective-permute-start.6 = (f32[9,24,96]{2,1,0:T(8,128)S(1)}, f32[9,24,96]{2,1,0:T(8,128)S(1)}, u32[]{:S(2)}, u32[]{:S(2)}) collective-permute-start(f32[9,24,96]{2,1,0:T(8,128)S(1)} %get-tuple-element.62), channel_id=1, source_target_pairs={{0,1},{1,0},{2,3},{3,2},{4,5},{5,4},{6,7},{7,6},{8,9},{9,8},{10,11... | collective-permute-start | bytes 248840 | tf_op jit(solution)/shard_map/ppermute | solution.py:450
  27.7 6.1 %collective-permute-start.7 = (f32[9,24,96]{2,1,0:T(8,128)S(1)}, f32[9,24,96]{2,1,0:T(8,128)S(1)}, u32[]{:S(2)}, u32[]{:S(2)}) collective-permute-start(f32[9,24,96]{2,1,0:T(8,128)S(1)} %get-tuple-element.63), channel_id=1, source_target_pairs={{1,2},{2,1},{5,6},{6,5},{9,10},{10,9},{13,14},{14,13},{17,18},{18,... | collective-permute-start | bytes 248840 | tf_op jit(solution)/shard_map/ppermute | solution.py:450

commit v5 on v4

--- a/solution.py
+++ b/solution.py
@@ -192,14 +192,14 @@
 
 
 def predict_kernel(axes, *refs):
-    sources, (stiff_ref, project_ref, lift_ref, sems), refs = refs[:12], refs[32:36], refs[12:32] + refs[36:]
-    first_ref, late_ref, s0, s1, s2, s3, w_ref, wo_ref, wa_ref, wl_ref = refs[:10]
-    kept, rest_ref, tiles = refs[10:19], refs[19], refs[20:]
-    dofs_ref, star_ref, lists_ref = kept[:3]
+    sources, (stiff_ref, sems), refs = refs[:12], refs[32:34], refs[12:32] + refs[34:]
+    first_ref, late_ref, s0, s1, s2, s3, w_ref, wo_ref = refs[:8]
+    kept, rest_ref, tiles = refs[8:19], refs[19], refs[20:]
+    project_ref, _, dofs_ref, star_ref, lists_ref = kept[:5]
     v_refs, t_refs = tiles[::2], tiles[1::2]
     h = step_length
     rows = first_ref.shape[1]
-    targets = (stiff_ref, project_ref, lift_ref) + tuple(kept)
+    targets = (stiff_ref,) + tuple(kept)
     copies = [pltpu.make_async_copy(src, dst, sems.at[i]) for i, (src, dst) in enumerate(zip(sources, targets))]
     for copy in copies:
         copy.start()
@@ -211,8 +211,6 @@
     height = w_ref.shape[0]
     wo_ref[:height] = series_weights(stiff_ref, rows, True)
     wo_ref[height:] = jnp.concatenate(block_weights(flat, rows, 3, False), axis=0).astype(bf16)
-    wa_ref[...] = across_weights(project_ref)
-    wl_ref[...] = lift_weights(lift_ref, rows)
     copies[3].wait()
     for q in range(dofs_ref.shape[0]):
         for i, v_ref in enumerate(v_refs):
@@ -315,8 +313,13 @@
     return [picked_ref.at[:, f * n : (f + 1) * n] for f in range(faces)]
 
 
-def own_kernel(own_ref, star_ref, rest_ref, minus_ref, w_ref, near_ref, face_ref, type_ref,
-               part_ref, g_ref, picked_ref, trace_ref, t_ref):
+def own_kernel(own_ref, star_ref, rest_ref, minus_ref, w_ref, near_ref, face_ref, type_ref, *refs):
+    if len(refs) > 5:
+        project_ref, lift_ref, part_ref, g_ref, picked_ref, wa_ref, wl_ref, trace_ref, t_ref = refs
+        wa_ref[...] = across_weights(project_ref)
+        wl_ref[...] = lift_weights(lift_ref, own_ref.shape[1])
+    else:
+        part_ref, g_ref, picked_ref, trace_ref, t_ref = refs
     quantities, rows, n = own_ref.shape
     tall = trace_ref.shape[1]
     groups = quantities // 3
@@ -489,27 +492,27 @@
     t_trace = pltpu.VMEM((quantities, tall, n), f32)
     picked = pltpu.VMEM((2 * quantities * rows, faces * n), f32)
 
-    local = (stiffness, project, lift)
-    kept = (dofs, star, send_list, minus, plus, neighbour, neighbour_face, face_type, cluster)
+    local = (stiffness,)
+    kept = (project, lift, dofs, star, send_list, minus, plus, neighbour, neighbour_face, face_type, cluster)
     inputs = local + kept
     first, late, *out = call(
         functools.partial(predict_kernel, axes), "predict", inputs,
-        (field, field, *sends, *weights, *(jax.ShapeDtypeStruct(a.shape, a.dtype) for a in kept),
+        (field, field, *sends, *weights[:2], *(jax.ShapeDtypeStruct(a.shape, a.dtype) for a in kept),
          jax.ShapeDtypeStruct((quantities, groups * len(rest_pairs()), 8, n), f32)),
         [pltpu.VMEM(a.shape, a.dtype) for a in local] + [pltpu.SemaphoreType.DMA((len(inputs),))] + tiles,
         10_000_000, far=range(len(inputs)))
-    out, (w, wo, wa, wl), kept = out[:DIRS], out[DIRS : 2 * DIRS], out[2 * DIRS :]
-    dofs, star, send_list, minus, plus, neighbour, neighbour_face, face_type, cluster, rest = kept
-
-    def own(buffer, name):
+    out, (w, wo), kept = out[:DIRS], out[DIRS : DIRS + 2], out[DIRS + 2 :]
+    project, lift, dofs, star, send_list, minus, plus, neighbour, neighbour_face, face_type, cluster, rest = kept
+
+    def own(buffer, name, more=(), made=()):
         return call(
-            own_kernel, name, (buffer, star, rest, minus, wo, neighbour, neighbour_face, face_type),
-            (field, traces, jax.ShapeDtypeStruct((2 * quantities * rows, faces * n), f32)),
+            own_kernel, name, (buffer, star, rest, minus, wo, neighbour, neighbour_face, face_type, *more),
+            (field, traces, jax.ShapeDtypeStruct((2 * quantities * rows, faces * n), f32), *made),
             [t_trace, t_field], 10_000_000)
 
     ghost_scratch = [picked, t_trace, t_trace]
     got = swap(out)
-    part, g, chosen = own(first, "own_first")
+    part, g, chosen, wa, wl = own(first, "own_first", (project, lift), weights[2:])
     midway, second, *out = call(
         functools.partial(middle_kernel, axes), "middle",
         (*got, plus, wa, wl, neighbour, neighbour_face, face_type, part, g, chosen, dofs, star, rest, w,

time: 36.8 us -> 36.3 us (0.986)
  waiting for transfers between devices: 0.86 us -> 0.3 us
    ppermute x8, waiting for transfers between devices: 0.86 us -> 0.3 us  [exchange(): return lax.ppermute(block, axis, route)]
  transfers between devices with their start and end apart: 8 -> 8, of which waited for: 2 -> 2; matrix products, arithmetic and copies ran while one was open for 0% -> 0% of each run, Pallas kernels for 13% -> 14%
where the time goes in v5:
time: 36.3 us; the launch traced here: 36.1 us
  Pallas kernels  18.8 us (52%)
  starting transfers between devices  16.8 us (46%)
    pallas_call x5, Pallas kernels, call(): pl.pallas_call(kernel, out_shape=[jax.ShapeDtypeStruct(s.shape, s.dtype)...  18.8 us
    ppermute x8, starting transfers between devices, exchange(): return lax.ppermute(block, axis, route)  16.8 us
  transfers between devices with their start and end apart: 8, of which 2 were waited for; matrix products, arithmetic and copies ran while one was open for 0% of the time, Pallas kernels for 14%

profile of v5, /device:TPU:13, one launch (start us, length us, event | category | flops | bytes accessed | tf_op | source)
XLA Modules:
  0.0 36.1 jit_solution(17359305258763310099)
XLA Ops:
  0.0 5.3 %predict.1 = (f32[9,24,384]{2,1,0:T(8,128)S(1)}, f32[9,24,384]{2,1,0:T(8,128)S(1)}, f32[9,24,96]{2,1,0:T(8,128)S(1)}, f32[9,24,96]{2,1,0:T(8,128)S(1)}, f32[9,24...) custom-call(f32[3,20,20]{2,1,0:T(8,128)} %refs_0_.1, ...), custom_call_target="tpu_custom_call" | custom-call | flops 10000000 | bytes 6426560 | tf_op jit(solution)/shard_map/predict/pallas_call | solution.py:436
  5.3 0.3 collective-permute-start
  5.6 4.1 %collective-permute-start.1 = (f32[9,24,96]{2,1,0:T(8,128)S(1)}, f32[9,24,96]{2,1,0:T(8,128)S(1)}, u32[]{:S(2)}, u32[]{:S(2)}) collective-permute-start(f32[9,24,96]{2,1,0:T(8,128)S(1)} %get-tuple-element.40), channel_id=1, source_target_pairs={{4,8},{8,4},{12,16},{16,12},{20,24},{24,20},{5,9},{9,5},{13,17},{1... | collective-permute-start | bytes 248840 | tf_op jit(solution)/shard_map/ppermute | solution.py:453
  9.7 1.3 %collective-permute-start.2 = (f32[9,24,96]{2,1,0:T(8,128)S(1)}, f32[9,24,96]{2,1,0:T(8,128)S(1)}, u32[]{:S(2)}, u32[]{:S(2)}) collective-permute-start(f32[9,24,96]{2,1,0:T(8,128)S(1)} %get-tuple-element.41), channel_id=1, source_target_pairs={{0,1},{1,0},{2,3},{3,2},{4,5},{5,4},{6,7},{7,6},{8,9},{9,8},{10,11... | collective-permute-start | bytes 248840 | tf_op jit(solution)/shard_map/ppermute | solution.py:453
  11.0 3.0 %collective-permute-start.3 = (f32[9,24,96]{2,1,0:T(8,128)S(1)}, f32[9,24,96]{2,1,0:T(8,128)S(1)}, u32[]{:S(2)}, u32[]{:S(2)}) collective-permute-start(f32[9,24,96]{2,1,0:T(8,128)S(1)} %get-tuple-element.42), channel_id=1, source_target_pairs={{1,2},{2,1},{5,6},{6,5},{9,10},{10,9},{13,14},{14,13},{17,18},{18,... | collective-permute-start | bytes 248840 | tf_op jit(solution)/shard_map/ppermute | solution.py:453
  14.0 2.9 %own_first.1 = (f32[9,24,384]{2,1,0:T(8,128)S(1)}, f32[9,40,384]{2,1,0:T(8,128)S(1)}, f32[432,1536]{1,0:T(8,128)S(1)}, bf16[160,240]{1,0:T(8,128)(2,1)S(1)}, bf16[48,240]{1,0:T(8,128)(2,1)S(1)}) custom-call(f32[9,24,384]{2,1,0:T(8,128)S(1)} %get-tuple-element.44.own_ref, f32[9,9,3,384]{3,2,1,0:T(4,128)S(1)} %get-tuple-element.45.star_ref, ...), custom_call_target="tpu_custom_call" | custom-call | flops 10000000 | bytes 6887680 | tf_op jit(solution)/shard_map/own_first/pallas_call | solution.py:436
  16.9 0.0 collective-permute-done.got0
  16.9 0.0 collective-permute-done.1.got1
  16.9 0.0 collective-permute-done.2.got2
  16.9 0.1 collective-permute-done.3.got3
  17.1 5.6 %middle.1 = (f32[9,24,384]{2,1,0:T(8,128)S(1)}, f32[9,24,384]{2,1,0:T(8,128)S(1)}, f32[9,24,96]{2,1,0:T(8,128)S(1)}, f32[9,24,96]{2,1,0:T(8,128)S(1)}, f32[9,24,...) custom-call(f32[9,24,96]{2,1,0:T(8,128)S(1)} %collective-permute-done.got0, f32[9,24,96]{2,1,0:T(8,128)S(1)} %collective-permute-done.1.got1, ...), custom_call_target="tpu_custom_call" | custom-call | flops 10000000 | bytes 8384256 | tf_op jit(solution)/shard_map/middle/pallas_call | solution.py:436
  22.7 0.1 collective-permute-start.4
  22.8 4.4 %collective-permute-start.5 = (f32[9,24,96]{2,1,0:T(8,128)S(1)}, f32[9,24,96]{2,1,0:T(8,128)S(1)}, u32[]{:S(2)}, u32[]{:S(2)}) collective-permute-start(f32[9,24,96]{2,1,0:T(8,128)S(1)} %get-tuple-element.65), channel_id=1, source_target_pairs={{4,8},{8,4},{12,16},{16,12},{20,24},{24,20},{5,9},{9,5},{13,17},{1... | collective-permute-start | bytes 248840 | tf_op jit(solution)/shard_map/ppermute | solution.py:453
  27.2 0.1 collective-permute-start.6
  27.2 3.6 %collective-permute-start.7 = (f32[9,24,96]{2,1,0:T(8,128)S(1)}, f32[9,24,96]{2,1,0:T(8,128)S(1)}, u32[]{:S(2)}, u32[]{:S(2)}) collective-permute-start(f32[9,24,96]{2,1,0:T(8,128)S(1)} %get-tuple-element.67), channel_id=1, source_target_pairs={{1,2},{2,1},{5,6},{6,5},{9,10},{10,9},{13,14},{14,13},{17,18},{18,... | collective-permute-start | bytes 248840 | tf_op jit(solution)/shard_map/ppermute | solution.py:453
  30.8 2.3 %own_second.1 = (f32[9,24,384]{2,1,0:T(8,128)S(1)}, f32[9,40,384]{2,1,0:T(8,128)S(1)}, f32[432,1536]{1,0:T(8,128)S(1)}) custom-call(f32[9,24,384]{2,1,0:T(8,128)S(1)} %get-tuple-element.68.own_ref, f32[9,9,3,384]{3,2,1,0:T(4,128)S(1)} %get-tuple-element.45.star_ref, f32[9,15,8,384]{3,2,1,0:T(8,128)S(1)} %get-tuple-element.46.rest_ref, ...), custom_call_target="tpu_custom_call" | custom-call | flops 10000000 | bytes 6681600 | tf_op jit(solution)/shard_map/own_second/pallas_call | solution.py:436
  33.1 0.0 collective-permute-done.4.got0
  33.1 0.0 collective-permute-done.5.got1
  33.2 0.0 collective-permute-done.6.got2
  33.2 0.1 collective-permute-done.7.got3
  33.3 2.8 %finish.1 = f32[9,20,384]{2,1,0:T(8,128)} custom-call(f32[9,24,96]{2,1,0:T(8,128)S(1)} %collective-permute-done.4.got0, f32[9,24,96]{2,1,0:T(8,128)S(1)} %collective-permute-done.5.got1, f32[9,24,96]{2,1,0:T(8,128)S(1)} %collective-permute-done.6.got2, f32[9,24,96]{2,1,0:T(8,128)S(1)} %collective-permute-done.7.got3, ...), custom_call_target="tpu_custom_call" | custom-call | flops 10000000 | bytes 5194752 | tf_op jit(solution)/shard_map/finish/pallas_call | solution.py:436
Async XLA Ops:
  5.3 11.6 %collective-permute-start = (f32[9,24,96]{2,1,0:T(8,128)S(1)}, f32[9,24,96]{2,1,0:T(8,128)S(1)}, u32[]{:S(2)}, u32[]{:S(2)}) collective-permute-start(f32[9,24,96]{2,1,0:T(8,128)S(1)} %get-tuple-element.39), channel_id=1, source_target_pairs={{0,4},{4,0},{8,12},{12,8},{16,20},{20,16},{24,28},{28,24},{1,5},{5... | collective-permute-start | bytes 248840 | tf_op jit(solution)/shard_map/ppermute | solution.py:453
  5.6 11.4 %collective-permute-start.1 = (f32[9,24,96]{2,1,0:T(8,128)S(1)}, f32[9,24,96]{2,1,0:T(8,128)S(1)}, u32[]{:S(2)}, u32[]{:S(2)}) collective-permute-start(f32[9,24,96]{2,1,0:T(8,128)S(1)} %get-tuple-element.40), channel_id=1, source_target_pairs={{4,8},{8,4},{12,16},{16,12},{20,24},{24,20},{5,9},{9,5},{13,17},{1... | collective-permute-start | bytes 248840 | tf_op jit(solution)/shard_map/ppermute | solution.py:453
  9.7 7.2 %collective-permute-start.2 = (f32[9,24,96]{2,1,0:T(8,128)S(1)}, f32[9,24,96]{2,1,0:T(8,128)S(1)}, u32[]{:S(2)}, u32[]{:S(2)}) collective-permute-start(f32[9,24,96]{2,1,0:T(8,128)S(1)} %get-tuple-element.41), channel_id=1, source_target_pairs={{0,1},{1,0},{2,3},{3,2},{4,5},{5,4},{6,7},{7,6},{8,9},{9,8},{10,11... | collective-permute-start | bytes 248840 | tf_op jit(solution)/shard_map/ppermute | solution.py:453
  11.0 6.1 %collective-permute-start.3 = (f32[9,24,96]{2,1,0:T(8,128)S(1)}, f32[9,24,96]{2,1,0:T(8,128)S(1)}, u32[]{:S(2)}, u32[]{:S(2)}) collective-permute-start(f32[9,24,96]{2,1,0:T(8,128)S(1)} %get-tuple-element.42), channel_id=1, source_target_pairs={{1,2},{2,1},{5,6},{6,5},{9,10},{10,9},{13,14},{14,13},{17,18},{18,... | collective-permute-start | bytes 248840 | tf_op jit(solution)/shard_map/ppermute | solution.py:453
  22.7 10.4 %collective-permute-start.4 = (f32[9,24,96]{2,1,0:T(8,128)S(1)}, f32[9,24,96]{2,1,0:T(8,128)S(1)}, u32[]{:S(2)}, u32[]{:S(2)}) collective-permute-start(f32[9,24,96]{2,1,0:T(8,128)S(1)} %get-tuple-element.64), channel_id=1, source_target_pairs={{0,4},{4,0},{8,12},{12,8},{16,20},{20,16},{24,28},{28,24},{1,5},{5... | collective-permute-start | bytes 248840 | tf_op jit(solution)/shard_map/ppermute | solution.py:453
  22.8 10.4 %collective-permute-start.5 = (f32[9,24,96]{2,1,0:T(8,128)S(1)}, f32[9,24,96]{2,1,0:T(8,128)S(1)}, u32[]{:S(2)}, u32[]{:S(2)}) collective-permute-start(f32[9,24,96]{2,1,0:T(8,128)S(1)} %get-tuple-element.65), channel_id=1, source_target_pairs={{4,8},{8,4},{12,16},{16,12},{20,24},{24,20},{5,9},{9,5},{13,17},{1... | collective-permute-start | bytes 248840 | tf_op jit(solution)/shard_map/ppermute | solution.py:453
  27.2 6.0 %collective-permute-start.6 = (f32[9,24,96]{2,1,0:T(8,128)S(1)}, f32[9,24,96]{2,1,0:T(8,128)S(1)}, u32[]{:S(2)}, u32[]{:S(2)}) collective-permute-start(f32[9,24,96]{2,1,0:T(8,128)S(1)} %get-tuple-element.66), channel_id=1, source_target_pairs={{0,1},{1,0},{2,3},{3,2},{4,5},{5,4},{6,7},{7,6},{8,9},{9,8},{10,11... | collective-permute-start | bytes 248840 | tf_op jit(solution)/shard_map/ppermute | solution.py:453
  27.2 6.1 %collective-permute-start.7 = (f32[9,24,96]{2,1,0:T(8,128)S(1)}, f32[9,24,96]{2,1,0:T(8,128)S(1)}, u32[]{:S(2)}, u32[]{:S(2)}) collective-permute-start(f32[9,24,96]{2,1,0:T(8,128)S(1)} %get-tuple-element.67), channel_id=1, source_target_pairs={{1,2},{2,1},{5,6},{6,5},{9,10},{10,9},{13,14},{14,13},{17,18},{18,... | collective-permute-start | bytes 248840 | tf_op jit(solution)/shard_map/ppermute | solution.py:453
